TPU v7x, 1024 devices: a whole 4x8x16 slice. The times are simulated.
1024 devices in a mesh: seq: 64 (over x, y, core), chan: 16 (over z).
Axes of the slice: x: 4, y: 8, z: 16, core: 2. Of those that a mesh axis runs over, the one named last changes fastest.
Arguments:
- hyena_query: float32 [8192, 8192], P('chan', 'seq'), may hold values from -6 to 6
- hyena_key: float32 [8192, 8192], P('chan', 'seq'), may hold values from -6 to 6
- hyena_value: float32 [8192, 8192], P('chan', 'seq'), may hold values from -6 to 6
- long_filter: float32 [8192, 8192], P('chan', 'seq'), may hold values from -1.1 to 1.1
- queries: float32 [8192, 8192], P('seq', 'chan'), may hold values from -10 to 10
- keys: float32 [8192, 8192], P('seq', 'chan'), may hold values from -10 to 10
- key_blocks: int32 [64, 4], P('seq'), may hold values from -1 to 63, as said below
Outputs:
- hyena_out: float32 [8192, 8192], P('chan', 'seq')
- attended: float32 [8192, 8192], P('seq', 'chan')
Inputs may be any that keep to these rules, and one draw needn't show every extreme that they name: `key_blocks`: row i lists block i itself and up to 3 distinct other blocks among i - 3 .. i - 1, in any order; unused entries are -1. How many blocks a row lists varies from row to row, and some row lists 4.
All inputs are finite; a program needn't handle non-finite values.
Results may differ from a plain program's by a relative error of at most 0.0003.
Values sent between devices are 32-bit elements; how exact they have to be, the bound alone decides.
A program may use at most 32 MiB of HBM per device.

v0:
```python
import math

import jax
import jax.numpy as jnp
from jax import lax
from jax.sharding import PartitionSpec as P

HEAD_DIM = 128


EXACT = lax.Precision.HIGHEST


def shifted(block, axis, distance):
    devices = range(lax.axis_size(axis))
    route = [(i - distance, i) for i in devices if i - distance in devices]
    return lax.ppermute(block, axis, route)


def unit_table(rows_count, cols_count, modulus):
    index = (
        jnp.arange(rows_count, dtype=jnp.int32)[:, None]
        * jnp.arange(cols_count, dtype=jnp.int32)[None, :]
        % modulus
    )
    angle = index.astype(jnp.float32) * (2.0 * math.pi / modulus)
    return (jnp.cos(angle), jnp.sin(angle))


def factor_pair(total):
    inner = 1
    for candidate in range(1, math.isqrt(total) + 1):
        if total % candidate == 0:
            inner = candidate
    outer = total // inner
    if outer % 2 == 1:
        outer, inner = (inner, outer)
    return (outer, inner)


def finish_sections(real_part, imag_part, tables):
    first_cos, first_sin, twist_cos, twist_sin, last_cos, last_sin = tables
    turned_real = real_part * twist_cos + imag_part * twist_sin
    turned_imag = imag_part * twist_cos - real_part * twist_sin
    spec_real = jnp.einsum("kcb,bd->kcd", turned_real, last_cos, precision=EXACT) + jnp.einsum(
        "kcb,bd->kcd", turned_imag, last_sin, precision=EXACT
    )
    spec_imag = jnp.einsum("kcb,bd->kcd", turned_imag, last_cos, precision=EXACT) - jnp.einsum(
        "kcb,bd->kcd", turned_real, last_sin, precision=EXACT
    )
    return (spec_real, spec_imag)


def forward_spectrum(signal, tables, outer, inner):
    first_cos, first_sin = (tables[0], tables[1])
    count = signal.shape[0]
    halved = signal.reshape(count, outer // 2, inner)
    real_part = jnp.einsum("ca,kab->kcb", first_cos[:, : outer // 2], halved, precision=EXACT)
    imag_part = -jnp.einsum("ca,kab->kcb", first_sin[:, : outer // 2], halved, precision=EXACT)
    return finish_sections(real_part, imag_part, tables)


def inverse_spectrum(spec_real, spec_imag, tables, outer, inner):
    first_cos, first_sin, twist_cos, twist_sin, last_cos, last_sin = tables
    count = spec_real.shape[0]
    mixed_real = jnp.einsum("kcd,db->kcb", spec_real, last_cos, precision=EXACT) - jnp.einsum(
        "kcd,db->kcb", spec_imag, last_sin, precision=EXACT
    )
    mixed_imag = jnp.einsum("kcd,db->kcb", spec_imag, last_cos, precision=EXACT) + jnp.einsum(
        "kcd,db->kcb", spec_real, last_sin, precision=EXACT
    )
    back_real = mixed_real * twist_cos - mixed_imag * twist_sin
    back_imag = mixed_imag * twist_cos + mixed_real * twist_sin
    upper_cos = first_cos[:, : outer // 2]
    upper_sin = first_sin[:, : outer // 2]
    signal = jnp.einsum("ca,kcb->kab", upper_cos, back_real, precision=EXACT) - jnp.einsum(
        "ca,kcb->kab", upper_sin, back_imag, precision=EXACT
    )
    return signal.reshape(count, outer // 2 * inner) / (outer * inner)


def body(hyena_query, hyena_key, hyena_value, long_filter, queries, keys, key_blocks):
    channels, tokens = hyena_key.shape
    groups = lax.axis_size("seq")
    per_peer = channels // groups
    outer, inner = factor_pair(2 * tokens * groups)
    first_cos, first_sin = unit_table(outer, outer, outer)
    twist_cos, twist_sin = unit_table(outer, inner, outer * inner)
    last_cos, last_sin = unit_table(inner, inner, inner)
    tables = (first_cos, first_sin, twist_cos, twist_sin, last_cos, last_sin)

    def shaped(array):
        return array.reshape(groups, per_peer, tokens)

    gated_input = shaped(hyena_key * hyena_value)
    gated = lax.all_to_all(gated_input, "seq", split_axis=0, concat_axis=2, tiled=True)[0]
    filt = lax.all_to_all(shaped(long_filter), "seq", split_axis=0, concat_axis=2, tiled=True)[0]
    signal_real, signal_imag = forward_spectrum(gated, tables, outer, inner)
    filter_real, filter_imag = forward_spectrum(filt, tables, outer, inner)
    product_real = signal_real * filter_real - signal_imag * filter_imag
    product_imag = signal_real * filter_imag + signal_imag * filter_real
    result = inverse_spectrum(product_real, product_imag, tables, outer, inner)[None]
    mixed = lax.all_to_all(result, "seq", split_axis=2, concat_axis=0, tiled=True)
    hyena_out = hyena_query * mixed.reshape(channels, tokens)
    values = jnp.transpose(hyena_out)
    length, width = queries.shape
    heads_here = width // HEAD_DIM
    span = key_blocks.shape[1]
    paired = jnp.stack([keys, values])
    collected = [paired]
    carried = paired
    for offset in range(1, span):
        carried = shifted(carried, "seq", 1)
        collected.append(carried)
    received = jnp.stack(collected)
    key_rows = received[:, 0].reshape(span * length, heads_here, HEAD_DIM)
    value_rows = received[:, 1].reshape(span * length, heads_here, HEAD_DIM)
    me_index = lax.axis_index("seq")
    offsets = jnp.arange(span, dtype=jnp.int32)
    source = me_index - offsets
    active = jnp.any(key_blocks[0][None, :] == source[:, None], axis=1) & (source >= 0)
    token_positions = jnp.arange(length, dtype=jnp.int32)
    allowed = active[None, :, None] & (
        (offsets[None, :, None] > 0)
        | (token_positions[None, None, :] <= token_positions[:, None, None])
    )
    allowed = allowed.reshape(length, span * length)
    query_rows = queries.reshape(length, heads_here, HEAD_DIM)
    scores = jnp.einsum("qhd,khd->hqk", query_rows, key_rows, precision=EXACT) * HEAD_DIM ** (-0.5)
    scores = jnp.where(allowed[None], scores, -1e30)
    top = jnp.max(scores, axis=-1, keepdims=True)
    expo = jnp.exp(scores - top)
    weights = expo / jnp.sum(expo, axis=-1, keepdims=True)
    attended = jnp.einsum("hqk,khd->qhd", weights, value_rows, precision=EXACT).reshape(
        length, width
    )
    return (hyena_out, attended)


def solution(mesh):
    placed = (
        P("chan", "seq"),
        P("chan", "seq"),
        P("chan", "seq"),
        P("chan", "seq"),
        P("seq", "chan"),
        P("seq", "chan"),
        P("seq", None),
    )
    return jax.shard_map(
        body,
        mesh=mesh,
        in_specs=placed,
        out_specs=(P("chan", "seq"), P("seq", "chan")),
        check_vma=False,
    )
```

profile of v0, /device:TPU:6, one launch (start us, length us, event | category | flops | bytes accessed | tf_op | source)
XLA Modules:
  0.0 182.4 jit_solution(18191800896223727585)
XLA Ops:
  0.6 17.6 %all-to-all-start.1 = ((f32[64,8,128]{2,1,0:T(8,128)}), f32[64,8,128]{2,1,0:T(8,128)S(1)}, u32[]{:S(2)}, u32[]{:S(2)}) async-start(f32[64,8,128]{2,1,0:T(8,128)} %bitcast.145), calls=%async_computation.1 | async-start | bytes 524288 | tf_op jit(solution)/shard_map/all_to_all | solution.py:97
  19.3 1.8 multiply_bitcast_fusion
  21.1 8.8 %all-to-all-done.1 = f32[64,8,128]{2,1,0:T(8,128)S(1)} async-done(((f32[64,8,128]{2,1,0:T(8,128)}), f32[64,8,128]{2,1,0:T(8,128)S(1)}, u32[]{:S(2)}, u32[]{:S(2)}) %all-to-all-start.1) | async-done | bytes 262176 | tf_op jit(solution)/shard_map/all_to_all | solution.py:97
  29.9 6.7 %all-to-all-start = ((f32[64,8,128]{2,1,0:T(8,128)}), f32[64,8,128]{2,1,0:T(8,128)S(1)}, u32[]{:S(2)}, u32[]{:S(2)}) async-start(f32[64,8,128]{2,1,0:T(8,128)} %multiply_bitcast_fusion), calls=%async_computation | async-start | bytes 524288 | tf_op jit(solution)/shard_map/all_to_all | solution.py:96
  39.4 8.5 %all-to-all-done = f32[64,8,128]{2,1,0:T(8,128)S(1)} async-done(((f32[64,8,128]{2,1,0:T(8,128)}), f32[64,8,128]{2,1,0:T(8,128)S(1)}, u32[]{:S(2)}, u32[]{:S(2)}) %all-to-all-start) | async-done | bytes 262176 | tf_op jit(solution)/shard_map/all_to_all | solution.py:96
  47.9 1.0 convolution_bitcast_fusion
  48.9 1.0 fusion.2
  49.9 1.2 fusion.40
  51.1 1.2 fusion.41
  54.0 1.2 convolution_add_fusion.2
  55.2 1.2 multiply_subtract_fusion
  56.4 0.9 fusion.54
  57.3 1.1 fusion.52
  58.4 0.9 convolution_subtract_fusion
  59.3 0.9 convolution_add_fusion
  61.7 2.6 %copy.176 = f32[8,64,128]{0,2,1:T(8,128)} copy(f32[8,64,128]{2,1,0:T(8,128)S(1)} %fusion.4) | data formatting | bytes 524288 | tf_op jit(solution)/shard_map/div | solution.py:79
  64.8 38.4 %reduce = f32[8192,8]{1,0:T(8,128)} reduce(f32[8192,1,8]{2,1,0:T(1,128)} %bitcast.138, f32[]{:T(128)} %broadcast.228), dimensions={1}, to_apply=%bitcast.124.reduce_sub_computation | reduce | bytes 524292
  103.2 4.5 %reshape.155 = f32[64,1,1024]{2,1,0:T(1,128)} reshape(f32[8192,8]{1,0:T(8,128)} %reduce) | data formatting | bytes 524288
  107.7 6.5 %all-to-all-start.2 = ((f32[64,1,1024]{2,1,0:T(1,128)}), f32[64,1,1024]{2,1,0:T(1,128)S(1)}, u32[]{:S(2)}, u32[]{:S(2)}) async-start(f32[64,1,1024]{2,1,0:T(1,128)} %reshape.155), calls=%async_computation.2 | async-start | bytes 524288 | tf_op jit(solution)/shard_map/all_to_all | solution.py:103
  114.3 11.4 %all-to-all-done.2 = f32[64,1,1024]{2,1,0:T(1,128)S(1)} async-done(((f32[64,1,1024]{2,1,0:T(1,128)}), f32[64,1,1024]{2,1,0:T(1,128)S(1)}, u32[]{:S(2)}, u32[]{:S(2)}) %all-to-all-start.2) | async-done | bytes 262176 | tf_op jit(solution)/shard_map/all_to_all | solution.py:103
  125.8 1.3 reduce.1
  127.0 8.4 %reshape.156 = f32[8192,1,8]{2,1,0:T(1,128)} reshape(f32[64,1024]{1,0:T(8,128)S(1)} %reduce.1) | data formatting | bytes 524288
  135.4 2.8 %copy.133 = f32[64,1,8,128]{3,2,0,1:T(8,128)S(1)} copy(f32[64,1,8,128]{2,3,0,1:T(8,128)} %bitcast.139) | data formatting | bytes 524288 | tf_op jit(solution)/shard_map/all_to_all | solution.py:103
  139.1 2.0 %collective-permute-start = (f32[2,128,512]{1,2,0:T(8,128)S(1)}, f32[2,128,512]{1,2,0:T(8,128)S(1)}, u32[]{:S(2)}, u32[]{:S(2)}) collective-permute-start(f32[2,128,512]{1,2,0:T(8,128)S(1)} %get-tuple-element.15), channel_id=1, source_target_pairs={{0,16},{16,32},{32,48},{48,64},{64,80},{80,96},{96,112},{112,128},... | collective-permute-start | bytes 1572872 | tf_op jit(solution)/shard_map/ppermute | solution.py:17
  141.1 10.6 %collective-permute-done = f32[2,128,512]{1,2,0:T(8,128)S(1)} collective-permute-done((f32[2,128,512]{1,2,0:T(8,128)S(1)}, f32[2,128,512]{1,2,0:T(8,128)S(1)}, u32[]{:S(2)}, u32[]{:S(2)}) %collective-permute-start) | collective-permute-done | bytes 524320 | tf_op jit(solution)/shard_map/ppermute | solution.py:17
  151.7 1.9 %collective-permute-start.1 = (f32[2,128,512]{1,2,0:T(8,128)S(1)}, f32[2,128,512]{1,2,0:T(8,128)S(1)}, u32[]{:S(2)}, u32[]{:S(2)}) collective-permute-start(f32[2,128,512]{1,2,0:T(8,128)S(1)} %collective-permute-done), channel_id=1, source_target_pairs={{0,16},{16,32},{32,48},{48,64},{64,80},{80,96},{96,112},{112,128},... | collective-permute-start | bytes 1572872 | tf_op jit(solution)/shard_map/ppermute | solution.py:17
  153.8 10.4 %collective-permute-done.1 = f32[2,128,512]{1,2,0:T(8,128)S(1)} collective-permute-done((f32[2,128,512]{1,2,0:T(8,128)S(1)}, f32[2,128,512]{1,2,0:T(8,128)S(1)}, u32[]{:S(2)}, u32[]{:S(2)}) %collective-permute-start.1) | collective-permute-done | bytes 524320 | tf_op jit(solution)/shard_map/ppermute | solution.py:17
  164.3 1.9 %collective-permute-start.2 = (f32[2,128,512]{1,2,0:T(8,128)S(1)}, f32[2,128,512]{1,2,0:T(8,128)S(1)}, u32[]{:S(2)}, u32[]{:S(2)}) collective-permute-start(f32[2,128,512]{1,2,0:T(8,128)S(1)} %collective-permute-done.1), channel_id=1, source_target_pairs={{0,16},{16,32},{32,48},{48,64},{64,80},{80,96},{96,112},{112,128},... | collective-permute-start | bytes 1572872 | tf_op jit(solution)/shard_map/ppermute | solution.py:17
  166.5 10.4 %collective-permute-done.2 = f32[2,128,512]{1,2,0:T(8,128)S(1)} collective-permute-done((f32[2,128,512]{1,2,0:T(8,128)S(1)}, f32[2,128,512]{1,2,0:T(8,128)S(1)}, u32[]{:S(2)}, u32[]{:S(2)}) %collective-permute-start.2) | collective-permute-done | bytes 524320 | tf_op jit(solution)/shard_map/ppermute | solution.py:17
  179.0 1.1 fusion.133
  180.3 1.3 fusion.6
  181.6 0.8 copy.140
  (41 shorter events, 11.3 us)
Async XLA Ops:
  0.6 178.4 %copy-start = (f32[128,512]{1,0:T(8,128)S(1)}, f32[128,512]{1,0:T(8,128)}, u32[]{:S(2)}) copy-start(f32[128,512]{1,0:T(8,128)} %param.11) | copy-start | bytes 786436
  0.6 29.2 %all-to-all-start.1 = ((f32[64,8,128]{2,1,0:T(8,128)}), f32[64,8,128]{2,1,0:T(8,128)S(1)}, u32[]{:S(2)}, u32[]{:S(2)}) async-start(f32[64,8,128]{2,1,0:T(8,128)} %bitcast.145), calls=%async_computation.1 | async-start | bytes 524288 | tf_op jit(solution)/shard_map/all_to_all | solution.py:97
  29.9 18.0 %all-to-all-start = ((f32[64,8,128]{2,1,0:T(8,128)}), f32[64,8,128]{2,1,0:T(8,128)S(1)}, u32[]{:S(2)}, u32[]{:S(2)}) async-start(f32[64,8,128]{2,1,0:T(8,128)} %multiply_bitcast_fusion), calls=%async_computation | async-start | bytes 524288 | tf_op jit(solution)/shard_map/all_to_all | solution.py:96
  103.2 11.0 %copy-start.3 = (f32[128,512]{1,0:T(8,128)S(1)}, f32[128,512]{1,0:T(8,128)}, u32[]{:S(2)}) copy-start(f32[128,512]{1,0:T(8,128)} %param.12) | copy-start | bytes 786436
  107.7 18.0 %all-to-all-start.2 = ((f32[64,1,1024]{2,1,0:T(1,128)}), f32[64,1,1024]{2,1,0:T(1,128)S(1)}, u32[]{:S(2)}, u32[]{:S(2)}) async-start(f32[64,1,1024]{2,1,0:T(1,128)} %reshape.155), calls=%async_computation.2 | async-start | bytes 524288 | tf_op jit(solution)/shard_map/all_to_all | solution.py:103
  135.4 2.8 %copy-start.2 = (f32[512,128]{1,0:T(8,128)S(1)}, f32[512,128]{1,0:T(8,128)}, u32[]{:S(2)}) copy-start(f32[512,128]{1,0:T(8,128)} %param.7) | copy-start | bytes 786436
  138.2 15.4 %copy-start.4 = (s32[1,4]{1,0:T(1,128)S(1)}, s32[1,4]{1,0:T(1,128)}, u32[]{:S(2)}) copy-start(s32[1,4]{1,0:T(1,128)} %param.13) | copy-start | bytes 52
  138.3 0.7 copy-start.1
  139.1 12.6 %collective-permute-start = (f32[2,128,512]{1,2,0:T(8,128)S(1)}, f32[2,128,512]{1,2,0:T(8,128)S(1)}, u32[]{:S(2)}, u32[]{:S(2)}) collective-permute-start(f32[2,128,512]{1,2,0:T(8,128)S(1)} %get-tuple-element.15), channel_id=1, source_target_pairs={{0,16},{16,32},{32,48},{48,64},{64,80},{80,96},{96,112},{112,128},... | collective-permute-start | bytes 1572872 | tf_op jit(solution)/shard_map/ppermute | solution.py:17
  151.7 12.6 %collective-permute-start.1 = (f32[2,128,512]{1,2,0:T(8,128)S(1)}, f32[2,128,512]{1,2,0:T(8,128)S(1)}, u32[]{:S(2)}, u32[]{:S(2)}) collective-permute-start(f32[2,128,512]{1,2,0:T(8,128)S(1)} %collective-permute-done), channel_id=1, source_target_pairs={{0,16},{16,32},{32,48},{48,64},{64,80},{80,96},{96,112},{112,128},... | collective-permute-start | bytes 1572872 | tf_op jit(solution)/shard_map/ppermute | solution.py:17
  164.3 12.6 %collective-permute-start.2 = (f32[2,128,512]{1,2,0:T(8,128)S(1)}, f32[2,128,512]{1,2,0:T(8,128)S(1)}, u32[]{:S(2)}, u32[]{:S(2)}) collective-permute-start(f32[2,128,512]{1,2,0:T(8,128)S(1)} %collective-permute-done.1), channel_id=1, source_target_pairs={{0,16},{16,32},{32,48},{48,64},{64,80},{80,96},{96,112},{112,128},... | collective-permute-start | bytes 1572872 | tf_op jit(solution)/shard_map/ppermute | solution.py:17
where the time goes:
time: 183 us; the launch traced here: 182 us
  waiting for transfers between devices  60 us (33%)
  other arithmetic  43.1 us (24%)
  starting transfers between devices  36.6 us (20%)
  local copies, waits for them, and re-layouts  22.7 us (12%)
  matrix products  19 us (10%)
    unnamed x1, other arithmetic  38.4 us
    ppermute x3, waiting for transfers between devices, shifted(): return lax.ppermute(block, axis, route)  31.4 us
    all_to_all x1, starting transfers between devices, body(): lax.all_to_all(shaped(long_filter), 'seq', split_axis=0, concat_axis=2, t...  17.6 us
    unnamed x15, local copies, waits for them, and re-layouts  15.1 us
    all_to_all x1, waiting for transfers between devices, body(): lax.all_to_all(result, 'seq', split_axis=2, concat_axis=0, tiled=True)  11.4 us
    all_to_all x1, waiting for transfers between devices, body(): lax.all_to_all(shaped(long_filter), 'seq', split_axis=0, concat_axis=2, t...  8.79 us
    all_to_all x1, waiting for transfers between devices, body(): lax.all_to_all(gated_input, 'seq', split_axis=0, concat_axis=2, tiled=True)  8.46 us
    all_to_all x1, starting transfers between devices, body(): lax.all_to_all(gated_input, 'seq', split_axis=0, concat_axis=2, tiled=True)  6.65 us
  transfers between devices with their start and end apart: 6, of which 6 were waited for; matrix products, arithmetic and copies ran while one was open for 3% of the time, Pallas kernels for 0%

commit v1 on v0

v1 whole, which is shorter than its diff:
```python
import functools

import jax
import jax.numpy as jnp
import numpy as np
from jax import lax
from jax.experimental import pallas as pl
from jax.experimental.pallas import tpu as pltpu
from jax.sharding import PartitionSpec as P

HEAD_DIM = 128
EXACT = lax.Precision.HIGHEST
CHANNELS = 8


def split(value):
    high = value.astype(jnp.bfloat16)
    low = (value - high.astype(jnp.float32)).astype(jnp.bfloat16)
    return high, low


def dot(left, right):
    return jnp.dot(left, right, preferred_element_type=jnp.float32)


def dot_nt(left, right, precision=None):
    return lax.dot_general(
        left,
        right,
        (((1,), (1,)), ((), ())),
        precision=precision,
        preferred_element_type=jnp.float32,
    )


def split_table(table):
    high = table.astype(np.float32).astype(jnp.bfloat16)
    low = (table - high.astype(np.float64)).astype(np.float32).astype(jnp.bfloat16)
    return high, low


def transform_tables(groups, length):
    total = 2 * groups * length
    half = np.arange(groups)[:, None] + 0.5
    first = 2 * np.pi * half * np.arange(groups)[None, :] / (2 * groups)
    twist = 2 * np.pi * half * np.arange(length)[None, :] / total
    last = 2 * np.pi * np.arange(length)[:, None] * np.arange(length)[None, :] / length
    ahead = np.concatenate([np.cos(first), -np.sin(first)], axis=0)
    back = ahead.T * (2.0 / total)
    ahead_high, ahead_low = split_table(ahead)
    back_high, back_low = split_table(back)
    cosine, sine = np.cos(last), np.sin(last)
    forward = np.block([[cosine, -sine], [sine, cosine]])
    inverse = np.block([[cosine, sine], [-sine, cosine]])
    return (
        np.concatenate([ahead_high, ahead_high, ahead_low], axis=1),
        np.concatenate([back_high, back_high, back_low], axis=1),
        np.stack([np.cos(twist), np.sin(twist)]).astype(np.float32),
        np.stack(split_table(forward)),
        np.stack(split_table(inverse)),
    )


def three_pass(high_ref, low_ref, table_ref):
    high = high_ref[...]
    return dot(high, table_ref[0]) + dot(low_ref[...], table_ref[0]) + dot(high, table_ref[1])


def to_spectrum(block, ahead, twist, forward, high_ref, low_ref):
    groups, length = twist.shape[1:]
    twist_cos, twist_sin = twist[0], twist[1]
    for pair in range(CHANNELS // 2):
        high, low = split(jnp.concatenate([block(2 * pair), block(2 * pair + 1)], axis=1))
        mixed = dot(ahead[...], jnp.concatenate([high, low, high], axis=0))
        for side in range(2):
            real = mixed[:groups, side * length : (side + 1) * length]
            imag = mixed[groups:, side * length : (side + 1) * length]
            turned = jnp.concatenate(
                [real * twist_cos + imag * twist_sin, imag * twist_cos - real * twist_sin], axis=1
            )
            high, low = split(turned)
            rows = pl.ds((2 * pair + side) * groups, groups)
            high_ref[rows, :] = high
            low_ref[rows, :] = low
    return three_pass(high_ref, low_ref, forward)


def multiply_back(spectrum, other, back, twist, inverse, high_ref, low_ref, store):
    groups, length = twist.shape[1:]
    real = spectrum[:, :length] * other[:, :length] - spectrum[:, length:] * other[:, length:]
    imag = spectrum[:, :length] * other[:, length:] + spectrum[:, length:] * other[:, :length]
    high_ref[...], low_ref[...] = split(jnp.concatenate([real, imag], axis=1))
    mixed = three_pass(high_ref, low_ref, inverse)
    twist_cos, twist_sin = twist[0], twist[1]

    def turned(channel):
        part = mixed[channel * groups : (channel + 1) * groups]
        real, imag = part[:, :length], part[:, length:]
        return jnp.concatenate(
            [real * twist_cos - imag * twist_sin, imag * twist_cos + real * twist_sin], axis=0
        )

    for pair in range(CHANNELS // 2):
        high, low = split(jnp.concatenate([turned(2 * pair), turned(2 * pair + 1)], axis=1))
        signal = dot(back[...], jnp.concatenate([high, low, high], axis=0))
        store(2 * pair, signal[:, :length])
        store(2 * pair + 1, signal[:, length:])


def convolve_kernel(received, ahead, back, twist, forward, inverse, result, high, low, spectrum):
    groups = twist.shape[1]

    def block(which):
        return lambda k: received[pl.ds(which * CHANNELS + k, groups, stride=2 * CHANNELS), :]

    def store(k, value):
        result[pl.ds(k, groups, stride=CHANNELS), :] = value

    spectrum[...] = to_spectrum(block(1), ahead, twist, forward, high, low)
    signal = to_spectrum(block(0), ahead, twist, forward, high, low)
    multiply_back(signal, spectrum[...], back, twist, inverse, high, low, store)


def allowed_keys(key_blocks, source, offset, length):
    listed = jnp.max((key_blocks == source).astype(jnp.float32), axis=1, keepdims=True)
    listed = jnp.where(source >= 0, listed, 0.0) > 0.5
    if offset:
        return jnp.broadcast_to(listed, (length, length))
    rows = lax.broadcasted_iota(jnp.int32, (length, length), 0)
    cols = lax.broadcasted_iota(jnp.int32, (length, length), 1)
    return jnp.broadcast_to(listed, (length, length)) & (cols <= rows)


def attend_kernel(queries, key_blocks, *refs):
    keys, values, result = refs[:4], refs[4:8], refs[8]
    length, width = queries.shape
    span = len(keys)
    me = lax.axis_index("seq")
    allowed = [allowed_keys(key_blocks[...], me - o, o, length) for o in range(span)]
    for head in range(width // HEAD_DIM):
        cols = slice(head * HEAD_DIM, (head + 1) * HEAD_DIM)
        query = queries[:, cols] * HEAD_DIM ** (-0.5)
        scores = [
            jnp.where(allowed[o], dot_nt(query, keys[o][:, cols], EXACT), -1e30) for o in range(span)
        ]
        top = functools.reduce(jnp.maximum, scores)
        top = jnp.max(top, axis=1, keepdims=True)
        expo = [jnp.exp(s - top) for s in scores]
        total = jnp.sum(functools.reduce(jnp.add, expo), axis=1, keepdims=True)
        high, low = split(jnp.concatenate(expo, axis=1))
        value_high, value_low = split(jnp.concatenate([values[o][cols, :] for o in range(span)], axis=1))
        out = dot_nt(high, value_high) + dot_nt(low, value_high) + dot_nt(high, value_low)
        result[:, cols] = out / total


def call(kernel, shape, scratch, operands):
    return pl.pallas_call(
        kernel,
        out_shape=jax.ShapeDtypeStruct(shape, jnp.float32),
        in_specs=[pl.BlockSpec(memory_space=pltpu.VMEM)] * len(operands),
        out_specs=pl.BlockSpec(memory_space=pltpu.VMEM),
        scratch_shapes=scratch,
    )(*operands)


def from_before(array, distance):
    size = lax.axis_size("seq")
    return lax.ppermute(array, "seq", [(i, i + distance) for i in range(size - distance)])


def body(hyena_query, hyena_key, hyena_value, long_filter, queries, keys, key_blocks):
    channels, length = hyena_key.shape
    groups = lax.axis_size("seq")
    span = key_blocks.shape[1]
    shape = (groups, CHANNELS, length)
    sent = jnp.concatenate(
        [(hyena_key * hyena_value).reshape(shape), long_filter.reshape(shape)], axis=1
    )
    received = lax.all_to_all(sent, "seq", split_axis=0, concat_axis=0, tiled=True)
    tables = [jnp.asarray(t) for t in transform_tables(groups, length)]
    rows = CHANNELS * groups
    convolved = call(
        convolve_kernel,
        (rows, length),
        [
            pltpu.VMEM((rows, 2 * length), jnp.bfloat16),
            pltpu.VMEM((rows, 2 * length), jnp.bfloat16),
            pltpu.VMEM((rows, 2 * length), jnp.float32),
        ],
        [received.reshape(2 * rows, length), *tables],
    )
    mixed = lax.all_to_all(
        convolved.reshape(shape), "seq", split_axis=0, concat_axis=0, tiled=True
    )
    hyena_out = hyena_query * mixed.reshape(channels, length)
    all_keys = [keys] + [from_before(keys, o) for o in range(1, span)]
    all_values = [hyena_out] + [from_before(hyena_out, o) for o in range(1, span)]
    attended = call(
        attend_kernel, queries.shape, [], [queries, key_blocks, *all_keys, *all_values]
    )
    return (hyena_out, attended)


def solution(mesh):
    placed = (
        P("chan", "seq"),
        P("chan", "seq"),
        P("chan", "seq"),
        P("chan", "seq"),
        P("seq", "chan"),
        P("seq", "chan"),
        P("seq", None),
    )
    return jax.shard_map(
        body,
        mesh=mesh,
        in_specs=placed,
        out_specs=(P("chan", "seq"), P("seq", "chan")),
        check_vma=False,
    )
```

time: 183 us -> 96.8 us (0.53)
  other arithmetic: 43.1 us -> 1.17 us
  blocking collectives: 0 us -> 34.1 us
  waiting for transfers between devices: 60 us -> 26.2 us
  local copies, waits for them, and re-layouts: 22.7 us -> 0.75 us
  matrix products: 19 us -> 0 us
  starting transfers between devices: 36.6 us -> 23.8 us
  Pallas kernels: 0 us -> 9.53 us
    unnamed x1 -> x0, other arithmetic: 38.4 us -> none
    all_to_all x0 -> x1, blocking collectives: none -> 34.1 us  [body(): lax.all_to_all(sent, 'seq', split_axis=0, concat_axis=0, tiled=True)]
    all_to_all x3 -> x1, waiting for transfers between devices: 28.7 us -> 1.92 us  [body(): lax.all_to_all(convolved.reshape(shape), 'seq', split_axis=0, concat_axis...]
    all_to_all x3 -> x1, starting transfers between devices: 30.8 us -> 7.02 us  [body(): lax.all_to_all(convolved.reshape(shape), 'seq', split_axis=0, concat_axis...]
    dot_general x20 -> x0, matrix products: 19 us -> none  [the longest x2 2.02 us: finish_sections(): jnp.einsum('kcb,bd->kcd', turned_real, last_sin, precision=EXACT)]
    unnamed x15 -> x20, local copies, waits for them, and re-layouts: 15.1 us -> 0.75 us
    ppermute x3 -> x6, starting transfers between devices: 5.86 us -> 16.8 us  [from_before(): lax.ppermute(array, 'seq', [(i, i + distance) for i in range(size - dista...]
    pallas_call x0 -> x2, Pallas kernels: none -> 9.53 us  [call(): pl.pallas_call(kernel, out_shape=jax.ShapeDtypeStruct(shape, jnp.float32)...]
  transfers between devices with their start and end apart: 6 -> 7, of which waited for: 6 -> 6; matrix products, arithmetic and copies ran while one was open for 3% -> 0% of each run, Pallas kernels for 0% -> 0%
where the time goes in v1:
time: 96.8 us; the launch traced here: 96.3 us
  blocking collectives  34.1 us (35%)
  waiting for transfers between devices  26.2 us (27%)
  starting transfers between devices  23.8 us (25%)
  Pallas kernels  9.53 us (10%)
  other arithmetic  1.17 us (1%)
    all_to_all x1, blocking collectives, body(): lax.all_to_all(sent, 'seq', split_axis=0, concat_axis=0, tiled=True)  34.1 us
    ppermute x6, waiting for transfers between devices, from_before(): lax.ppermute(array, 'seq', [(i, i + distance) for i in range(size - dista...  24.2 us
    ppermute x6, starting transfers between devices, from_before(): lax.ppermute(array, 'seq', [(i, i + distance) for i in range(size - dista...  16.8 us
    pallas_call x2, Pallas kernels, call(): pl.pallas_call(kernel, out_shape=jax.ShapeDtypeStruct(shape, jnp.float32)...  9.53 us
    all_to_all x1, starting transfers between devices, body(): lax.all_to_all(convolved.reshape(shape), 'seq', split_axis=0, concat_axis...  7.02 us
  transfers between devices with their start and end apart: 7, of which 6 were waited for; matrix products, arithmetic and copies ran while one was open for 0% of the time, Pallas kernels for 0%

profile of v1, /device:TPU:6, one launch (start us, length us, event | category | flops | bytes accessed | tf_op | source)
XLA Modules:
  0.0 96.3 jit_solution(9670591783672470568)
XLA Ops:
  0.6 0.0 copy-start.2
  0.6 1.1 %multiply_bitcast_fusion = f32[64,8,128]{2,1,0:T(8,128)S(1)} fusion(f32[512,128]{1,0:T(8,128)} %param.13, f32[512,128]{1,0:T(8,128)} %param.14), kind=kLoop, calls=%fused_computation.2 | loop fusion | flops 65536 | bytes 786432 | tf_op jit(solution)/shard_map/reshape | solution.py:177
  1.7 0.0 copy-done.2
  1.8 34.1 %all_to_all.10 = f32[64,16,128]{2,1,0:T(8,128)} all-to-all(f32[64,16,128]{2,1,0:T(8,128)S(1)} %pad_maximum_fusion), channel_id=1, replica_groups=mesh['seq'=64,'chan'=16] {'seq'}, dimensions={0} | all-to-all | bytes 1048576 | tf_op jit(solution)/shard_map/all_to_all | solution.py:179
  35.9 3.6 %shard_map.131 = f32[512,128]{1,0:T(8,128)} custom-call(f32[1024,128]{1,0:T(8,128)} %bitcast.7, bf16[128,192]{1,0:T(8,128)(2,1)} %constant.10.clone.ahead, bf16[64,384]{1,0:T(8,128)(2,1)} %constant.11.clone.back, f32[2,64,128]{2,1,0:T(8,128)} %constant.12.clone.twist, bf16[2,256,256]{2,1,0:T(8,128)(2,1)} %constant.13.clone.forward, ...), custom_call_target="tpu_custom_call" | custom-call | tf_op jit(solution)/shard_map/pallas_call | solution.py:157
  39.5 7.0 %all-to-all-start.1 = ((f32[64,8,128]{2,1,0:T(8,128)}), f32[64,8,128]{2,1,0:T(8,128)S(1)}, u32[]{:S(2)}, u32[]{:S(2)}) async-start(f32[64,8,128]{2,1,0:T(8,128)} %bitcast.8), calls=%async_computation.1 | async-start | bytes 524288 | tf_op jit(solution)/shard_map/all_to_all | solution.py:192
  46.5 0.0 copy-done.3
  46.6 3.4 %collective-permute-start.1 = (f32[128,512]{1,0:T(8,128)S(1)}, f32[128,512]{1,0:T(8,128)S(1)}, u32[]{:S(2)}, u32[]{:S(2)}) collective-permute-start(f32[128,512]{1,0:T(8,128)S(1)} %copy-done.3), channel_id=1, source_target_pairs={{0,32},{16,48},{32,64},{48,80},{64,96},{80,112},{96,128},{112,144}... | collective-permute-start | bytes 786440 | tf_op jit(solution)/shard_map/ppermute | solution.py:168
  50.0 1.9 %collective-permute-start = (f32[128,512]{1,0:T(8,128)S(1)}, f32[128,512]{1,0:T(8,128)S(1)}, u32[]{:S(2)}, u32[]{:S(2)}) collective-permute-start(f32[128,512]{1,0:T(8,128)S(1)} %copy-done.3), channel_id=1, source_target_pairs={{0,16},{16,32},{32,48},{48,64},{64,80},{80,96},{96,112},{112,128},... | collective-permute-start | bytes 786440 | tf_op jit(solution)/shard_map/ppermute | solution.py:168
  51.9 4.6 %collective-permute-start.2 = (f32[128,512]{1,0:T(8,128)S(1)}, f32[128,512]{1,0:T(8,128)S(1)}, u32[]{:S(2)}, u32[]{:S(2)}) collective-permute-start(f32[128,512]{1,0:T(8,128)S(1)} %copy-done.3), channel_id=1, source_target_pairs={{0,48},{16,64},{32,80},{48,96},{64,112},{80,128},{96,144},{112,160... | collective-permute-start | bytes 786440 | tf_op jit(solution)/shard_map/ppermute | solution.py:168
  56.5 1.9 %all-to-all-done.1 = f32[64,8,128]{2,1,0:T(8,128)S(1)} async-done(((f32[64,8,128]{2,1,0:T(8,128)}), f32[64,8,128]{2,1,0:T(8,128)S(1)}, u32[]{:S(2)}, u32[]{:S(2)}) %all-to-all-start.1) | async-done | bytes 262176 | tf_op jit(solution)/shard_map/all_to_all | solution.py:192
  58.4 0.0 copy-done.1
  58.4 0.0 copy-start
  58.4 2.2 %collective-permute-start.5 = (f32[512,128]{1,0:T(8,128)S(1)}, f32[512,128]{1,0:T(8,128)S(1)}, u32[]{:S(2)}, u32[]{:S(2)}) collective-permute-start(f32[512,128]{1,0:T(8,128)S(1)} %bitcast_multiply_fusion.refs_4_), channel_id=1, source_target_pairs={{0,48},{16,64},{32,80},{48,96},{64,112},{80,128},{96,144},{112,160... | collective-permute-start | bytes 786440 | tf_op jit(solution)/shard_map/ppermute | solution.py:168
  60.6 2.5 %collective-permute-start.4 = (f32[512,128]{1,0:T(8,128)S(1)}, f32[512,128]{1,0:T(8,128)S(1)}, u32[]{:S(2)}, u32[]{:S(2)}) collective-permute-start(f32[512,128]{1,0:T(8,128)S(1)} %bitcast_multiply_fusion.refs_4_), channel_id=1, source_target_pairs={{0,32},{16,48},{32,64},{48,80},{64,96},{80,112},{96,128},{112,144}... | collective-permute-start | bytes 786440 | tf_op jit(solution)/shard_map/ppermute | solution.py:168
  63.1 0.0 collective-permute-done.1.refs_2_
  63.1 0.0 copy-start.4
  63.1 2.3 %collective-permute-start.3 = (f32[512,128]{1,0:T(8,128)S(1)}, f32[512,128]{1,0:T(8,128)S(1)}, u32[]{:S(2)}, u32[]{:S(2)}) collective-permute-start(f32[512,128]{1,0:T(8,128)S(1)} %bitcast_multiply_fusion.refs_4_), channel_id=1, source_target_pairs={{0,16},{16,32},{32,48},{48,64},{64,80},{80,96},{96,112},{112,128},... | collective-permute-start | bytes 786440 | tf_op jit(solution)/shard_map/ppermute | solution.py:168
  65.4 1.3 %collective-permute-done.refs_1_ = f32[128,512]{1,0:T(8,128)S(1)} collective-permute-done((f32[128,512]{1,0:T(8,128)S(1)}, f32[128,512]{1,0:T(8,128)S(1)}, u32[]{:S(2)}, u32[]{:S(2)}) %collective-permute-start) | collective-permute-done | bytes 262176 | tf_op jit(solution)/shard_map/ppermute | solution.py:168
  66.7 9.1 %collective-permute-done.2.refs_3_ = f32[128,512]{1,0:T(8,128)S(1)} collective-permute-done((f32[128,512]{1,0:T(8,128)S(1)}, f32[128,512]{1,0:T(8,128)S(1)}, u32[]{:S(2)}, u32[]{:S(2)}) %collective-permute-start.2) | collective-permute-done | bytes 262176 | tf_op jit(solution)/shard_map/ppermute | solution.py:168
  75.9 8.4 %collective-permute-done.5.refs_7_ = f32[512,128]{1,0:T(8,128)S(1)} collective-permute-done((f32[512,128]{1,0:T(8,128)S(1)}, f32[512,128]{1,0:T(8,128)S(1)}, u32[]{:S(2)}, u32[]{:S(2)}) %collective-permute-start.5) | collective-permute-done | bytes 262176 | tf_op jit(solution)/shard_map/ppermute | solution.py:168
  84.3 0.2 collective-permute-done.4.refs_6_
  84.5 5.1 %collective-permute-done.3.refs_5_ = f32[512,128]{1,0:T(8,128)S(1)} collective-permute-done((f32[512,128]{1,0:T(8,128)S(1)}, f32[512,128]{1,0:T(8,128)S(1)}, u32[]{:S(2)}, u32[]{:S(2)}) %collective-permute-start.3) | collective-permute-done | bytes 262176 | tf_op jit(solution)/shard_map/ppermute | solution.py:168
  89.7 0.0 copy-done
  89.7 0.0 copy-done.4
  89.7 0.0 copy-done.5
  89.7 0.0 copy-done.6
  89.7 0.0 copy-done.7
  89.7 0.0 copy-done.8
  89.7 0.0 copy-start.9
  89.7 0.7 copy-done.9
  90.4 5.9 %shard_map.132 = f32[128,512]{1,0:T(8,128)} custom-call(f32[128,512]{1,0:T(8,128)} %queries.1, s32[1,4]{1,0:T(1,128)} %key_blocks.1, f32[128,512]{1,0:T(8,128)} %refs_0_.1, f32[128,512]{1,0:T(8,128)} %copy-done.5, f32[128,512]{1,0:T(8,128)} %copy-done.4, f32[128,512]{1,0:T(8,128)} %copy-done.6, f32[512,128]{1,0:T(8,128)} %copy-done, f32[512,128]{1,0:T(8,128)} %copy-done.9, ...), custom_call_target="tpu_custom_call" | custom-call | tf_op jit(solution)/shard_map/pallas_call | solution.py:157
  (8 shorter events, 0.1 us)
Async XLA Ops:
  0.6 1.1 %copy-start.2 = (f32[512,128]{1,0:T(8,128)S(1)}, f32[512,128]{1,0:T(8,128)}, u32[]{:S(2)}) copy-start(f32[512,128]{1,0:T(8,128)} %param.15) | copy-start | bytes 786436
  39.5 7.0 %copy-start.3 = (f32[128,512]{1,0:T(8,128)S(1)}, f32[128,512]{1,0:T(8,128)}, u32[]{:S(2)}) copy-start(f32[128,512]{1,0:T(8,128)} %refs_0_.1) | copy-start | bytes 786436
  39.5 18.9 %copy-start.1 = (f32[512,128]{1,0:T(8,128)S(1)}, f32[512,128]{1,0:T(8,128)}, u32[]{:S(2)}) copy-start(f32[512,128]{1,0:T(8,128)} %param.12) | copy-start | bytes 786436
  39.5 18.9 %all-to-all-start.1 = ((f32[64,8,128]{2,1,0:T(8,128)}), f32[64,8,128]{2,1,0:T(8,128)S(1)}, u32[]{:S(2)}, u32[]{:S(2)}) async-start(f32[64,8,128]{2,1,0:T(8,128)} %bitcast.8), calls=%async_computation.1 | async-start | bytes 524288 | tf_op jit(solution)/shard_map/all_to_all | solution.py:192
  46.6 16.5 %collective-permute-start.1 = (f32[128,512]{1,0:T(8,128)S(1)}, f32[128,512]{1,0:T(8,128)S(1)}, u32[]{:S(2)}, u32[]{:S(2)}) collective-permute-start(f32[128,512]{1,0:T(8,128)S(1)} %copy-done.3), channel_id=1, source_target_pairs={{0,32},{16,48},{32,64},{48,80},{64,96},{80,112},{96,128},{112,144}... | collective-permute-start | bytes 786440 | tf_op jit(solution)/shard_map/ppermute | solution.py:168
  50.0 16.8 %collective-permute-start = (f32[128,512]{1,0:T(8,128)S(1)}, f32[128,512]{1,0:T(8,128)S(1)}, u32[]{:S(2)}, u32[]{:S(2)}) collective-permute-start(f32[128,512]{1,0:T(8,128)S(1)} %copy-done.3), channel_id=1, source_target_pairs={{0,16},{16,32},{32,48},{48,64},{64,80},{80,96},{96,112},{112,128},... | collective-permute-start | bytes 786440 | tf_op jit(solution)/shard_map/ppermute | solution.py:168
  51.9 24.0 %collective-permute-start.2 = (f32[128,512]{1,0:T(8,128)S(1)}, f32[128,512]{1,0:T(8,128)S(1)}, u32[]{:S(2)}, u32[]{:S(2)}) collective-permute-start(f32[128,512]{1,0:T(8,128)S(1)} %copy-done.3), channel_id=1, source_target_pairs={{0,48},{16,64},{32,80},{48,96},{64,112},{80,128},{96,144},{112,160... | collective-permute-start | bytes 786440 | tf_op jit(solution)/shard_map/ppermute | solution.py:168
  58.4 31.3 %copy-start = (f32[512,128]{1,0:T(8,128)}, f32[512,128]{1,0:T(8,128)S(1)}, u32[]{:S(2)}) copy-start(f32[512,128]{1,0:T(8,128)S(1)} %bitcast_multiply_fusion.refs_4_) | copy-start | bytes 786436
  58.4 25.9 %collective-permute-start.5 = (f32[512,128]{1,0:T(8,128)S(1)}, f32[512,128]{1,0:T(8,128)S(1)}, u32[]{:S(2)}, u32[]{:S(2)}) collective-permute-start(f32[512,128]{1,0:T(8,128)S(1)} %bitcast_multiply_fusion.refs_4_), channel_id=1, source_target_pairs={{0,48},{16,64},{32,80},{48,96},{64,112},{80,128},{96,144},{112,160... | collective-permute-start | bytes 786440 | tf_op jit(solution)/shard_map/ppermute | solution.py:168
  60.6 23.9 %collective-permute-start.4 = (f32[512,128]{1,0:T(8,128)S(1)}, f32[512,128]{1,0:T(8,128)S(1)}, u32[]{:S(2)}, u32[]{:S(2)}) collective-permute-start(f32[512,128]{1,0:T(8,128)S(1)} %bitcast_multiply_fusion.refs_4_), channel_id=1, source_target_pairs={{0,32},{16,48},{32,64},{48,80},{64,96},{80,112},{96,128},{112,144}... | collective-permute-start | bytes 786440 | tf_op jit(solution)/shard_map/ppermute | solution.py:168
  63.1 26.6 %copy-start.4 = (f32[128,512]{1,0:T(8,128)}, f32[128,512]{1,0:T(8,128)S(1)}, u32[]{:S(2)}) copy-start(f32[128,512]{1,0:T(8,128)S(1)} %collective-permute-done.1.refs_2_) | copy-start | bytes 786436
  63.1 26.6 %collective-permute-start.3 = (f32[512,128]{1,0:T(8,128)S(1)}, f32[512,128]{1,0:T(8,128)S(1)}, u32[]{:S(2)}, u32[]{:S(2)}) collective-permute-start(f32[512,128]{1,0:T(8,128)S(1)} %bitcast_multiply_fusion.refs_4_), channel_id=1, source_target_pairs={{0,16},{16,32},{32,48},{48,64},{64,80},{80,96},{96,112},{112,128},... | collective-permute-start | bytes 786440 | tf_op jit(solution)/shard_map/ppermute | solution.py:168
  66.7 23.0 %copy-start.5 = (f32[128,512]{1,0:T(8,128)}, f32[128,512]{1,0:T(8,128)S(1)}, u32[]{:S(2)}) copy-start(f32[128,512]{1,0:T(8,128)S(1)} %collective-permute-done.refs_1_) | copy-start | bytes 786436
  75.9 13.8 %copy-start.6 = (f32[128,512]{1,0:T(8,128)}, f32[128,512]{1,0:T(8,128)S(1)}, u32[]{:S(2)}) copy-start(f32[128,512]{1,0:T(8,128)S(1)} %collective-permute-done.2.refs_3_) | copy-start | bytes 786436
  84.3 5.4 %copy-start.7 = (f32[512,128]{1,0:T(8,128)}, f32[512,128]{1,0:T(8,128)S(1)}, u32[]{:S(2)}) copy-start(f32[512,128]{1,0:T(8,128)S(1)} %collective-permute-done.5.refs_7_) | copy-start | bytes 786436
  84.5 5.2 %copy-start.8 = (f32[512,128]{1,0:T(8,128)}, f32[512,128]{1,0:T(8,128)S(1)}, u32[]{:S(2)}) copy-start(f32[512,128]{1,0:T(8,128)S(1)} %collective-permute-done.4.refs_6_) | copy-start | bytes 786436
  89.7 0.7 copy-start.9

commit v2 on v1

--- a/solution.py
+++ b/solution.py
@@ -107,20 +107,6 @@
         store(2 * pair + 1, signal[:, length:])
 
 
-def convolve_kernel(received, ahead, back, twist, forward, inverse, result, high, low, spectrum):
-    groups = twist.shape[1]
-
-    def block(which):
-        return lambda k: received[pl.ds(which * CHANNELS + k, groups, stride=2 * CHANNELS), :]
-
-    def store(k, value):
-        result[pl.ds(k, groups, stride=CHANNELS), :] = value
-
-    spectrum[...] = to_spectrum(block(1), ahead, twist, forward, high, low)
-    signal = to_spectrum(block(0), ahead, twist, forward, high, low)
-    multiply_back(signal, spectrum[...], back, twist, inverse, high, low, store)
-
-
 def allowed_keys(key_blocks, source, offset, length):
     listed = jnp.max((key_blocks == source).astype(jnp.float32), axis=1, keepdims=True)
     listed = jnp.where(source >= 0, listed, 0.0) > 0.5
@@ -131,74 +117,239 @@
     return jnp.broadcast_to(listed, (length, length)) & (cols <= rows)
 
 
-def attend_kernel(queries, key_blocks, *refs):
-    keys, values, result = refs[:4], refs[4:8], refs[8]
-    length, width = queries.shape
-    span = len(keys)
+MESH = pl.DeviceIdType.MESH
+X, Y, CORES = 4, 8, 2
+GROUPS = X * Y * CORES
+WIDE = GROUPS // 4
+
+
+def peer_of(me, turn):
+    step = turn + turn // 58
+    core, way = step % 2, (step // 2) % 2
+    over, reach = (step // 4) % 4, (step // 16) % 4
+    along = (1 - way) * (4 + reach) + way * (3 - reach)
+    x, y = me // (Y * CORES), (me // CORES) % Y
+    return ((x + over + 2) % X * Y + (y + along) % Y) * CORES + (me + core) % CORES
+
+
+def to_all(source, target, me, send_sem, recv_sem):
+    mine = pl.ds(pl.multiple_of(me * CHANNELS, CHANNELS), CHANNELS)
+
+    def send(turn, carry):
+        peer = peer_of(me, turn)
+        rows = pl.ds(pl.multiple_of(peer * CHANNELS, CHANNELS), CHANNELS)
+        pltpu.make_async_remote_copy(
+            src_ref=source.at[rows, :],
+            dst_ref=target.at[mine, :],
+            send_sem=send_sem,
+            recv_sem=recv_sem,
+            device_id={"seq": peer},
+            device_id_type=MESH,
+        ).start()
+        return carry
+
+    lax.fori_loop(0, GROUPS - 1, send, 0)
+    pltpu.make_async_copy(source.at[mine, :], target.at[mine, :], recv_sem).start()
+
+
+def done(ref, sem):
+    pltpu.make_async_copy(ref, ref, sem).wait()
+
+
+def start_to(source, target, peer, send_sem, recv_sem):
+    pltpu.make_async_remote_copy(
+        src_ref=source,
+        dst_ref=target,
+        send_sem=send_sem,
+        recv_sem=recv_sem,
+        device_id={"seq": peer},
+        device_id_type=MESH,
+    ).start()
+
+
+def kernel(
+    query_hbm, key_hbm, value_hbm, filter_hbm, queries_hbm, keys_hbm, key_blocks,
+    ahead, back, twist, forward, inverse,
+    hyena, attended,
+    gate, gate_key, gate_value, taps, queries, keys, got_taps, got_gate, convolved, got_back,
+    values, high, low, spectrum, weight_high, weight_low,
+    load_sem, all_send, taps_sem, gate_sem, back_sem, key_send, key_recv, value_send, value_recv,
+):
+    groups, length = twist.shape[1:]
+    span = keys.shape[0]
+    heads = queries.shape[1] // HEAD_DIM
     me = lax.axis_index("seq")
+    core = me % CORES
+    after, later = (me + 1) % GROUPS, (me + 2) % GROUPS
+    barrier = pltpu.get_barrier_semaphore()
+
+    def greet(turn, carry):
+        pl.semaphore_signal(
+            barrier, inc=1, device_id={"seq": peer_of(me, turn)}, device_id_type=MESH
+        )
+        return carry
+
+    lax.fori_loop(0, GROUPS - 1, greet, 0)
+    loads = [
+        pltpu.make_async_copy(source, target, load_sem.at[i])
+        for i, (source, target) in enumerate(
+            [
+                (filter_hbm, taps),
+                (key_hbm, gate_key),
+                (value_hbm, gate_value),
+                (keys_hbm, keys.at[0]),
+                (queries_hbm, queries),
+                (query_hbm, gate),
+            ]
+        )
+    ]
+    for load in loads:
+        load.start()
+    loads[1].wait()
+    loads[2].wait()
+    gate_key[...] = gate_key[...] * gate_value[...]
+    loads[0].wait()
+    loads[3].wait()
+    pl.semaphore_wait(barrier, GROUPS - 1)
+
+    to_all(taps, got_taps, me, all_send.at[0], taps_sem)
+    to_all(gate_key, got_gate, me, all_send.at[1], gate_sem)
+
+    def block(ref):
+        return lambda k: ref[pl.ds(k, groups, stride=CHANNELS), :]
+
+    def store(k, value):
+        convolved[pl.ds(k, groups, stride=CHANNELS), :] = value
+
+    done(got_taps, taps_sem)
+    spectrum[...] = to_spectrum(block(got_taps), ahead, twist, forward, high, low)
+    done(got_gate, gate_sem)
+
+    def pass_on(own, slots, send_sems, recv_sems):
+        start_to(own, slots[2], later, send_sems[2], recv_sems[2])
+
+        @pl.when(core == 0)
+        def _():
+            start_to(own, slots[1], after, send_sems[1], recv_sems[1])
+
+    def relay(slots, send_sems, recv_sems):
+        done(slots[2], recv_sems[2])
+
+        @pl.when(core == 1)
+        def _():
+            start_to(slots[2], slots[1], me - 1, send_sems[1], recv_sems[1])
+
+        start_to(slots[2], slots[3], after, send_sems[3], recv_sems[3])
+
+    key_slots = [keys.at[o] for o in range(span)]
+    key_sends = [key_send.at[o] for o in range(span)]
+    key_recvs = [key_recv.at[o] for o in range(span)]
+    pass_on(key_slots[0], key_slots, key_sends, key_recvs)
+    signal = to_spectrum(block(got_gate), ahead, twist, forward, high, low)
+    multiply_back(signal, spectrum[...], back, twist, inverse, high, low, store)
+    to_all(convolved, got_back, me, all_send.at[2], back_sem.at[me // WIDE])
+    relay(key_slots, key_sends, key_recvs)
+    loads[4].wait()
+    loads[5].wait()
+
+    def part(head):
+        rows = pl.ds(head * HEAD_DIM, HEAD_DIM)
+        slots = [hyena.at[rows, :]] + [values.at[o, rows, :] for o in range(1, span)]
+        sends = [value_send.at[o, head] for o in range(span)]
+        recvs = [value_recv.at[o, head] for o in range(span)]
+        return rows, slots, sends, recvs
+
+    for head in range(heads):
+        rows, slots, sends, recvs = part(head)
+        done(got_back.at[rows, :], back_sem.at[head])
+        hyena[rows, :] = gate[rows, :] * got_back[rows, :]
+        pass_on(slots[0], slots, sends, recvs)
+
     allowed = [allowed_keys(key_blocks[...], me - o, o, length) for o in range(span)]
-    for head in range(width // HEAD_DIM):
+    done(key_slots[1], key_recvs[1])
+    done(key_slots[3], key_recvs[3])
+    for head in range(heads):
         cols = slice(head * HEAD_DIM, (head + 1) * HEAD_DIM)
         query = queries[:, cols] * HEAD_DIM ** (-0.5)
         scores = [
-            jnp.where(allowed[o], dot_nt(query, keys[o][:, cols], EXACT), -1e30) for o in range(span)
+            jnp.where(allowed[o], dot_nt(query, keys[o, :, cols], EXACT), -1e30) for o in range(span)
         ]
-        top = functools.reduce(jnp.maximum, scores)
-        top = jnp.max(top, axis=1, keepdims=True)
+        top = jnp.max(functools.reduce(jnp.maximum, scores), axis=1, keepdims=True)
         expo = [jnp.exp(s - top) for s in scores]
         total = jnp.sum(functools.reduce(jnp.add, expo), axis=1, keepdims=True)
-        high, low = split(jnp.concatenate(expo, axis=1))
-        value_high, value_low = split(jnp.concatenate([values[o][cols, :] for o in range(span)], axis=1))
-        out = dot_nt(high, value_high) + dot_nt(low, value_high) + dot_nt(high, value_low)
-        result[:, cols] = out / total
-
-
-def call(kernel, shape, scratch, operands):
-    return pl.pallas_call(
-        kernel,
-        out_shape=jax.ShapeDtypeStruct(shape, jnp.float32),
-        in_specs=[pl.BlockSpec(memory_space=pltpu.VMEM)] * len(operands),
-        out_specs=pl.BlockSpec(memory_space=pltpu.VMEM),
-        scratch_shapes=scratch,
-    )(*operands)
-
-
-def from_before(array, distance):
-    size = lax.axis_size("seq")
-    return lax.ppermute(array, "seq", [(i, i + distance) for i in range(size - distance)])
+        weight_high[head], weight_low[head] = split(jnp.concatenate(expo, axis=1) / total)
+        rows, slots, sends, recvs = part(head)
+        relay(slots, sends, recvs)
+
+    for head in range(heads):
+        rows, slots, sends, recvs = part(head)
+        done(slots[1], recvs[1])
+        done(slots[3], recvs[3])
+        value_high, value_low = split(jnp.concatenate([slot[...] for slot in slots], axis=1))
+        attended[:, head * HEAD_DIM : (head + 1) * HEAD_DIM] = (
+            dot_nt(weight_high[head], value_high)
+            + dot_nt(weight_low[head], value_high)
+            + dot_nt(weight_high[head], value_low)
+        )
+
+    others = (GROUPS - 1) * CHANNELS
+    for i, source in enumerate((taps, gate_key, convolved)):
+        done(source.at[pl.ds(0, others), :], all_send.at[i])
+    for o in range(1, span):
+        done(key_slots[o], key_sends[o])
+        for head in range(heads):
+            rows, slots, sends, recvs = part(head)
+            done(slots[o], sends[o])
 
 
 def body(hyena_query, hyena_key, hyena_value, long_filter, queries, keys, key_blocks):
     channels, length = hyena_key.shape
     groups = lax.axis_size("seq")
     span = key_blocks.shape[1]
-    shape = (groups, CHANNELS, length)
-    sent = jnp.concatenate(
-        [(hyena_key * hyena_value).reshape(shape), long_filter.reshape(shape)], axis=1
-    )
-    received = lax.all_to_all(sent, "seq", split_axis=0, concat_axis=0, tiled=True)
+    heads = queries.shape[1] // HEAD_DIM
     tables = [jnp.asarray(t) for t in transform_tables(groups, length)]
+    whole = pl.BlockSpec(memory_space=pl.ANY)
+    local = pl.BlockSpec(memory_space=pltpu.VMEM)
+    square = pltpu.VMEM((channels, length), jnp.float32)
+    dma = pltpu.SemaphoreType.DMA
     rows = CHANNELS * groups
-    convolved = call(
-        convolve_kernel,
-        (rows, length),
-        [
+    return pl.pallas_call(
+        kernel,
+        out_shape=(
+            jax.ShapeDtypeStruct(hyena_query.shape, jnp.float32),
+            jax.ShapeDtypeStruct(queries.shape, jnp.float32),
+        ),
+        in_specs=[whole] * 6 + [local] * (1 + len(tables)),
+        out_specs=(local, local),
+        scratch_shapes=[
+            square,
+            square,
+            square,
+            square,
+            pltpu.VMEM(queries.shape, jnp.float32),
+            pltpu.VMEM((span, *keys.shape), jnp.float32),
+            square,
+            square,
+            square,
+            square,
+            pltpu.VMEM((span, channels, length), jnp.float32),
             pltpu.VMEM((rows, 2 * length), jnp.bfloat16),
             pltpu.VMEM((rows, 2 * length), jnp.bfloat16),
             pltpu.VMEM((rows, 2 * length), jnp.float32),
+            pltpu.VMEM((heads, length, span * length), jnp.bfloat16),
+            pltpu.VMEM((heads, length, span * length), jnp.bfloat16),
+            dma((6,)),
+            dma((3,)),
+            dma,
+            dma,
+            dma((heads,)),
+            dma((span,)),
+            dma((span,)),
+            dma((span, heads)),
+            dma((span, heads)),
         ],
-        [received.reshape(2 * rows, length), *tables],
-    )
-    mixed = lax.all_to_all(
-        convolved.reshape(shape), "seq", split_axis=0, concat_axis=0, tiled=True
-    )
-    hyena_out = hyena_query * mixed.reshape(channels, length)
-    all_keys = [keys] + [from_before(keys, o) for o in range(1, span)]
-    all_values = [hyena_out] + [from_before(hyena_out, o) for o in range(1, span)]
-    attended = call(
-        attend_kernel, queries.shape, [], [queries, key_blocks, *all_keys, *all_values]
-    )
-    return (hyena_out, attended)
+        compiler_params=pltpu.CompilerParams(collective_id=0, has_side_effects=True),
+    )(hyena_query, hyena_key, hyena_value, long_filter, queries, keys, key_blocks, *tables)
 
 
 def solution(mesh):

time: 96.8 us -> 64.8 us (0.67)
  the two profiles are of different devices: /device:TPU:6 before, /device:TPU:1 now
where the time goes in v2:
time: 64.8 us; the launch traced here: 64.6 us
  Pallas kernels  61.5 us (95%)
  local copies, waits for them, and re-layouts  2.42 us (4%)
  between operations  0.65 us (1%)
    pallas_call x1, Pallas kernels, body(): pl.pallas_call(kernel, out_shape=(jax.ShapeDtypeStruct(hyena_query.shape,...  61.5 us
    unnamed x4, local copies, waits for them, and re-layouts  2.42 us

profile of v2, /device:TPU:1, one launch (start us, length us, event | category | flops | bytes accessed | tf_op | source)
XLA Modules:
  0.0 64.6 jit_solution(14839023330530550924)
XLA Ops:
  0.6 61.5 %shard_map.131 = (f32[512,128]{1,0:T(8,128)}, f32[128,512]{1,0:T(8,128)}) custom-call(f32[512,128]{1,0:T(8,128)} %query_hbm.1, f32[512,128]{1,0:T(8,128)} %key_hbm.1, f32[512,128]{1,0:T(8,128)} %value_hbm.1, f32[512,128]{1,0:T(8,128)} %filter_hbm.1, f32[128,512]{1,0:T(8,128)} %queries_hbm.1, f32[128,512]{1,0:T(8,128)} %keys_hbm.1, s32[1,4]{1,0:T(1,128)} %key_blocks.1, ...), custom_call_target="tpu_custom_call" | custom-call | tf_op jit(solution)/shard_map/pallas_call | solution.py:316
  62.2 0.0 copy-start
  62.2 1.7 %copy.16 = f32[512,128]{1,0:T(8,128)} copy(f32[512,128]{1,0:T(8,128)} %get-tuple-element.4) | data formatting | bytes 524288
  63.9 0.0 copy-done
  63.9 0.7 %copy.17 = f32[128,512]{1,0:T(8,128)} copy(f32[128,512]{1,0:T(8,128)S(1)} %copy-done) | data formatting | bytes 524288
Async XLA Ops:
  62.2 1.7 %copy-start = (f32[128,512]{1,0:T(8,128)S(1)}, f32[128,512]{1,0:T(8,128)}, u32[]{:S(2)}) copy-start(f32[128,512]{1,0:T(8,128)} %get-tuple-element.5) | copy-start | bytes 786436

commit v3 on v2

--- a/solution.py
+++ b/solution.py
@@ -120,35 +120,41 @@
 MESH = pl.DeviceIdType.MESH
 X, Y, CORES = 4, 8, 2
 GROUPS = X * Y * CORES
-WIDE = GROUPS // 4
-
-
-def peer_of(me, turn):
-    step = turn + turn // 58
-    core, way = step % 2, (step // 2) % 2
-    over, reach = (step // 4) % 4, (step // 16) % 4
-    along = (1 - way) * (4 + reach) + way * (3 - reach)
-    x, y = me // (Y * CORES), (me // CORES) % Y
-    return ((x + over + 2) % X * Y + (y + along) % Y) * CORES + (me + core) % CORES
-
-
-def to_all(source, target, me, send_sem, recv_sem):
+
+
+def terms(me):
+    x = lax.div(me, Y * CORES)
+    y = lax.rem(lax.div(me, CORES), Y)
+    core = lax.rem(me, CORES)
+    return x, [lax.rem(y + d, Y) * CORES for d in range(Y)], [core, 1 - core]
+
+
+def for_others(parts, act):
+    x, along, cores = parts
+    reach = [d for far in range(Y // 2, 0, -1) for d in dict.fromkeys((far, Y - far))] + [0]
+
+    def column(i, carry):
+        base = lax.rem(x + 1 + i, X) * (Y * CORES)
+        for d in reach:
+            for c in range(CORES):
+                act(base + along[d] + cores[c])
+        return carry
+
+    lax.fori_loop(0, X - 1, column, 0)
+    for d in reach:
+        for c in range(CORES):
+            if d or c:
+                act(x * (Y * CORES) + along[d] + cores[c])
+
+
+def to_all(source, target, me, parts, send_sem, recv_sem):
     mine = pl.ds(pl.multiple_of(me * CHANNELS, CHANNELS), CHANNELS)
 
-    def send(turn, carry):
-        peer = peer_of(me, turn)
+    def send(peer):
         rows = pl.ds(pl.multiple_of(peer * CHANNELS, CHANNELS), CHANNELS)
-        pltpu.make_async_remote_copy(
-            src_ref=source.at[rows, :],
-            dst_ref=target.at[mine, :],
-            send_sem=send_sem,
-            recv_sem=recv_sem,
-            device_id={"seq": peer},
-            device_id_type=MESH,
-        ).start()
-        return carry
-
-    lax.fori_loop(0, GROUPS - 1, send, 0)
+        start_to(source.at[rows, :], target.at[mine, :], peer, send_sem, recv_sem)
+
+    for_others(parts, send)
     pltpu.make_async_copy(source.at[mine, :], target.at[mine, :], recv_sem).start()
 
 
@@ -168,40 +174,37 @@
 
 
 def kernel(
-    query_hbm, key_hbm, value_hbm, filter_hbm, queries_hbm, keys_hbm, key_blocks,
-    ahead, back, twist, forward, inverse,
+    query_hbm, key_hbm, value_hbm, filter_hbm, queries_hbm, keys_hbm, key_blocks_hbm,
+    ahead_hbm, back_hbm, twist_hbm, forward_hbm, inverse_hbm,
     hyena, attended,
-    gate, gate_key, gate_value, taps, queries, keys, got_taps, got_gate, convolved, got_back,
-    values, high, low, spectrum, weight_high, weight_low,
+    gate, gate_key, gate_value, taps, queries, keys, key_blocks, ahead, back, twist, forward, inverse,
+    got_taps, got_gate, convolved, got_back, values, high, low, spectrum, weight_high, weight_low,
     load_sem, all_send, taps_sem, gate_sem, back_sem, key_send, key_recv, value_send, value_recv,
 ):
     groups, length = twist.shape[1:]
     span = keys.shape[0]
     heads = queries.shape[1] // HEAD_DIM
     me = lax.axis_index("seq")
-    core = me % CORES
-    after, later = (me + 1) % GROUPS, (me + 2) % GROUPS
+    parts = terms(me)
+    core = parts[2][0]
+    after, later = lax.rem(me + 1, GROUPS), lax.rem(me + 2, GROUPS)
     barrier = pltpu.get_barrier_semaphore()
 
-    def greet(turn, carry):
-        pl.semaphore_signal(
-            barrier, inc=1, device_id={"seq": peer_of(me, turn)}, device_id_type=MESH
-        )
-        return carry
-
-    lax.fori_loop(0, GROUPS - 1, greet, 0)
+    def greet(peer):
+        pl.semaphore_signal(barrier, inc=1, device_id={"seq": peer}, device_id_type=MESH)
+
+    for_others(parts, greet)
+    sources = [
+        filter_hbm, key_hbm, value_hbm, ahead_hbm, twist_hbm, forward_hbm,
+        keys_hbm, back_hbm, inverse_hbm, query_hbm, queries_hbm, key_blocks_hbm,
+    ]
+    targets = [
+        taps, gate_key, gate_value, ahead, twist, forward,
+        keys.at[0], back, inverse, gate, queries, key_blocks,
+    ]
     loads = [
         pltpu.make_async_copy(source, target, load_sem.at[i])
-        for i, (source, target) in enumerate(
-            [
-                (filter_hbm, taps),
-                (key_hbm, gate_key),
-                (value_hbm, gate_value),
-                (keys_hbm, keys.at[0]),
-                (queries_hbm, queries),
-                (query_hbm, gate),
-            ]
-        )
+        for i, (source, target) in enumerate(zip(sources, targets))
     ]
     for load in loads:
         load.start()
@@ -209,11 +212,12 @@
     loads[2].wait()
     gate_key[...] = gate_key[...] * gate_value[...]
     loads[0].wait()
-    loads[3].wait()
     pl.semaphore_wait(barrier, GROUPS - 1)
 
-    to_all(taps, got_taps, me, all_send.at[0], taps_sem)
-    to_all(gate_key, got_gate, me, all_send.at[1], gate_sem)
+    to_all(taps, got_taps, me, parts, all_send.at[0], taps_sem)
+    to_all(gate_key, got_gate, me, parts, all_send.at[1], gate_sem)
+    for load in loads[3:]:
+        load.wait()
 
     def block(ref):
         return lambda k: ref[pl.ds(k, groups, stride=CHANNELS), :]
@@ -247,10 +251,8 @@
     pass_on(key_slots[0], key_slots, key_sends, key_recvs)
     signal = to_spectrum(block(got_gate), ahead, twist, forward, high, low)
     multiply_back(signal, spectrum[...], back, twist, inverse, high, low, store)
-    to_all(convolved, got_back, me, all_send.at[2], back_sem.at[me // WIDE])
+    to_all(convolved, got_back, me, parts, all_send.at[2], back_sem.at[parts[0]])
     relay(key_slots, key_sends, key_recvs)
-    loads[4].wait()
-    loads[5].wait()
 
     def part(head):
         rows = pl.ds(head * HEAD_DIM, HEAD_DIM)
@@ -308,19 +310,18 @@
     span = key_blocks.shape[1]
     heads = queries.shape[1] // HEAD_DIM
     tables = [jnp.asarray(t) for t in transform_tables(groups, length)]
-    whole = pl.BlockSpec(memory_space=pl.ANY)
-    local = pl.BlockSpec(memory_space=pltpu.VMEM)
     square = pltpu.VMEM((channels, length), jnp.float32)
     dma = pltpu.SemaphoreType.DMA
     rows = CHANNELS * groups
+    operands = (hyena_query, hyena_key, hyena_value, long_filter, queries, keys, key_blocks, *tables)
     return pl.pallas_call(
         kernel,
         out_shape=(
-            jax.ShapeDtypeStruct(hyena_query.shape, jnp.float32),
-            jax.ShapeDtypeStruct(queries.shape, jnp.float32),
+            pltpu.VMEM(hyena_query.shape, jnp.float32),
+            pltpu.VMEM(queries.shape, jnp.float32),
         ),
-        in_specs=[whole] * 6 + [local] * (1 + len(tables)),
-        out_specs=(local, local),
+        in_specs=[pl.BlockSpec(memory_space=pltpu.HBM)] * len(operands),
+        out_specs=(pl.BlockSpec(memory_space=pltpu.VMEM), pl.BlockSpec(memory_space=pltpu.VMEM)),
         scratch_shapes=[
             square,
             square,
@@ -328,6 +329,8 @@
             square,
             pltpu.VMEM(queries.shape, jnp.float32),
             pltpu.VMEM((span, *keys.shape), jnp.float32),
+            pltpu.VMEM(key_blocks.shape, jnp.int32),
+            *[pltpu.VMEM(t.shape, t.dtype) for t in tables],
             square,
             square,
             square,
@@ -338,7 +341,7 @@
             pltpu.VMEM((rows, 2 * length), jnp.float32),
             pltpu.VMEM((heads, length, span * length), jnp.bfloat16),
             pltpu.VMEM((heads, length, span * length), jnp.bfloat16),
-            dma((6,)),
+            dma((len(operands),)),
             dma((3,)),
             dma,
             dma,
@@ -349,7 +352,7 @@
             dma((span, heads)),
         ],
         compiler_params=pltpu.CompilerParams(collective_id=0, has_side_effects=True),
-    )(hyena_query, hyena_key, hyena_value, long_filter, queries, keys, key_blocks, *tables)
+    )(*operands)
 
 
 def solution(mesh):

time: 64.8 us -> 60.7 us (0.937)
  Pallas kernels: 61.5 us -> 58.5 us
  local copies, waits for them, and re-layouts: 2.42 us -> 1.41 us
    pallas_call x1, Pallas kernels: 61.5 us -> 58.5 us  [body(): pl.pallas_call(kernel, out_shape=(pltpu.VMEM(hyena_query.shape, jnp.float...]
    unnamed x4 -> x2, local copies, waits for them, and re-layouts: 2.42 us -> 1.41 us
where the time goes in v3:
time: 60.7 us; the launch traced here: 60.5 us
  Pallas kernels  58.5 us (96%)
  local copies, waits for them, and re-layouts  1.41 us (2%)
  between operations  0.64 us (1%)
    pallas_call x1, Pallas kernels, body(): pl.pallas_call(kernel, out_shape=(pltpu.VMEM(hyena_query.shape, jnp.float...  58.5 us
    unnamed x2, local copies, waits for them, and re-layouts  1.41 us

profile of v3, /device:TPU:1, one launch (start us, length us, event | category | flops | bytes accessed | tf_op | source)
XLA Modules:
  0.0 60.5 jit_solution(4851008300053826810)
XLA Ops:
  0.6 58.5 %shard_map.131 = (f32[512,128]{1,0:T(8,128)S(1)}, f32[128,512]{1,0:T(8,128)S(1)}) custom-call(f32[512,128]{1,0:T(8,128)} %query_hbm.1, f32[512,128]{1,0:T(8,128)} %key_hbm.1, f32[512,128]{1,0:T(8,128)} %value_hbm.1, f32[512,128]{1,0:T(8,128)} %filter_hbm.1, f32[128,512]{1,0:T(8,128)} %queries_hbm.1, f32[128,512]{1,0:T(8,128)} %keys_hbm.1, ...), custom_call_target="tpu_custom_call" | custom-call | tf_op jit(solution)/shard_map/pallas_call | solution.py:317
  59.1 0.7 %copy.16 = f32[512,128]{1,0:T(8,128)} copy(f32[512,128]{1,0:T(8,128)S(1)} %get-tuple-element.2) | data formatting | bytes 524288
  59.8 0.7 %copy.17 = f32[128,512]{1,0:T(8,128)} copy(f32[128,512]{1,0:T(8,128)S(1)} %get-tuple-element.3) | data formatting | bytes 524288

commit v4 on v3

--- a/solution.py
+++ b/solution.py
@@ -147,12 +147,17 @@
                 act(x * (Y * CORES) + along[d] + cores[c])
 
 
-def to_all(source, target, me, parts, send_sem, recv_sem):
-    mine = pl.ds(pl.multiple_of(me * CHANNELS, CHANNELS), CHANNELS)
+def rows_of(device):
+    return pl.ds(pl.multiple_of(device * CHANNELS, CHANNELS), CHANNELS)
+
+
+def to_all(source, target, me, parts, send_sem, recv_sem, least=0):
+    mine = rows_of(me)
 
     def send(peer):
-        rows = pl.ds(pl.multiple_of(peer * CHANNELS, CHANNELS), CHANNELS)
-        start_to(source.at[rows, :], target.at[mine, :], peer, send_sem, recv_sem)
+        @pl.when(peer >= least)
+        def _():
+            start_to(source.at[rows_of(peer), :], target.at[mine, :], peer, send_sem, recv_sem)
 
     for_others(parts, send)
     pltpu.make_async_copy(source.at[mine, :], target.at[mine, :], recv_sem).start()
@@ -179,7 +184,7 @@
     hyena, attended,
     gate, gate_key, gate_value, taps, queries, keys, key_blocks, ahead, back, twist, forward, inverse,
     got_taps, got_gate, convolved, got_back, values, high, low, spectrum, weight_high, weight_low,
-    load_sem, all_send, taps_sem, gate_sem, back_sem, key_send, key_recv, value_send, value_recv,
+    here_sem, load_sem, all_send, taps_sem, gate_sem, back_sem, key_send, key_recv, value_send, value_recv,
 ):
     groups, length = twist.shape[1:]
     span = keys.shape[0]
@@ -193,7 +198,10 @@
     def greet(peer):
         pl.semaphore_signal(barrier, inc=1, device_id={"seq": peer}, device_id_type=MESH)
 
-    for_others(parts, greet)
+    @pl.when(me > 0)
+    def _():
+        for_others(parts, greet)
+
     sources = [
         filter_hbm, key_hbm, value_hbm, ahead_hbm, twist_hbm, forward_hbm,
         keys_hbm, back_hbm, inverse_hbm, query_hbm, queries_hbm, key_blocks_hbm,
@@ -212,10 +220,31 @@
     loads[2].wait()
     gate_key[...] = gate_key[...] * gate_value[...]
     loads[0].wait()
-    pl.semaphore_wait(barrier, GROUPS - 1)
-
-    to_all(taps, got_taps, me, parts, all_send.at[0], taps_sem)
-    to_all(gate_key, got_gate, me, parts, all_send.at[1], gate_sem)
+
+    @pl.when(me == 0)
+    def _():
+        pl.semaphore_wait(barrier, GROUPS - 1)
+        for_others(
+            parts,
+            lambda peer: pl.semaphore_signal(
+                here_sem, inc=1, device_id={"seq": peer}, device_id_type=MESH
+            ),
+        )
+
+    @pl.when(me > 0)
+    def _():
+        pl.semaphore_wait(barrier, GROUPS - 2)
+
+    to_all(taps, got_taps, me, parts, all_send.at[0], taps_sem, 1)
+    to_all(gate_key, got_gate, me, parts, all_send.at[1], gate_sem, 1)
+
+    @pl.when(me > 0)
+    def _():
+        pl.semaphore_wait(here_sem, 1)
+        mine = rows_of(me)
+        start_to(taps.at[rows_of(0), :], got_taps.at[mine, :], 0, all_send.at[0], taps_sem)
+        start_to(gate_key.at[rows_of(0), :], got_gate.at[mine, :], 0, all_send.at[1], gate_sem)
+
     for load in loads[3:]:
         load.wait()
 
@@ -224,10 +253,6 @@
 
     def store(k, value):
         convolved[pl.ds(k, groups, stride=CHANNELS), :] = value
-
-    done(got_taps, taps_sem)
-    spectrum[...] = to_spectrum(block(got_taps), ahead, twist, forward, high, low)
-    done(got_gate, gate_sem)
 
     def pass_on(own, slots, send_sems, recv_sems):
         start_to(own, slots[2], later, send_sems[2], recv_sems[2])
@@ -249,6 +274,10 @@
     key_sends = [key_send.at[o] for o in range(span)]
     key_recvs = [key_recv.at[o] for o in range(span)]
     pass_on(key_slots[0], key_slots, key_sends, key_recvs)
+    done(got_taps, taps_sem)
+    spectrum[...] = to_spectrum(block(got_taps), ahead, twist, forward, high, low)
+    done(got_gate, gate_sem)
+
     signal = to_spectrum(block(got_gate), ahead, twist, forward, high, low)
     multiply_back(signal, spectrum[...], back, twist, inverse, high, low, store)
     to_all(convolved, got_back, me, parts, all_send.at[2], back_sem.at[parts[0]])
@@ -341,6 +370,7 @@
             pltpu.VMEM((rows, 2 * length), jnp.float32),
             pltpu.VMEM((heads, length, span * length), jnp.bfloat16),
             pltpu.VMEM((heads, length, span * length), jnp.bfloat16),
+            pltpu.SemaphoreType.REGULAR,
             dma((len(operands),)),
             dma((3,)),
             dma,

time: 60.7 us -> 51.3 us (0.85)
  Pallas kernels: 58.5 us -> 49.1 us
    pallas_call x1, Pallas kernels: 58.5 us -> 49.1 us  [body(): pl.pallas_call(kernel, out_shape=(pltpu.VMEM(hyena_query.shape, jnp.float...]
where the time goes in v4:
time: 51.3 us; the launch traced here: 51.2 us
  Pallas kernels  49.1 us (96%)
  local copies, waits for them, and re-layouts  1.41 us (3%)
  between operations  0.64 us (1%)
    pallas_call x1, Pallas kernels, body(): pl.pallas_call(kernel, out_shape=(pltpu.VMEM(hyena_query.shape, jnp.float...  49.1 us
    unnamed x2, local copies, waits for them, and re-layouts  1.41 us

profile of v4, /device:TPU:1, one launch (start us, length us, event | category | flops | bytes accessed | tf_op | source)
XLA Modules:
  0.0 51.2 jit_solution(17361650106211028152)
XLA Ops:
  0.6 49.1 %shard_map.131 = (f32[512,128]{1,0:T(8,128)S(1)}, f32[128,512]{1,0:T(8,128)S(1)}) custom-call(f32[512,128]{1,0:T(8,128)} %query_hbm.1, f32[512,128]{1,0:T(8,128)} %key_hbm.1, f32[512,128]{1,0:T(8,128)} %value_hbm.1, f32[512,128]{1,0:T(8,128)} %filter_hbm.1, f32[128,512]{1,0:T(8,128)} %queries_hbm.1, f32[128,512]{1,0:T(8,128)} %keys_hbm.1, ...), custom_call_target="tpu_custom_call" | custom-call | tf_op jit(solution)/shard_map/pallas_call | solution.py:346
  49.8 0.7 %copy.16 = f32[512,128]{1,0:T(8,128)} copy(f32[512,128]{1,0:T(8,128)S(1)} %get-tuple-element.2) | data formatting | bytes 524288
  50.5 0.7 %copy.17 = f32[128,512]{1,0:T(8,128)} copy(f32[128,512]{1,0:T(8,128)S(1)} %get-tuple-element.3) | data formatting | bytes 524288

commit v5 on v4

--- a/solution.py
+++ b/solution.py
@@ -123,28 +123,27 @@
 
 
 def terms(me):
-    x = lax.div(me, Y * CORES)
-    y = lax.rem(lax.div(me, CORES), Y)
     core = lax.rem(me, CORES)
-    return x, [lax.rem(y + d, Y) * CORES for d in range(Y)], [core, 1 - core]
+    return lax.div(me, Y * CORES), lax.rem(lax.div(me, CORES), Y), [core, 1 - core]
 
 
 def for_others(parts, act):
-    x, along, cores = parts
-    reach = [d for far in range(Y // 2, 0, -1) for d in dict.fromkeys((far, Y - far))] + [0]
-
-    def column(i, carry):
-        base = lax.rem(x + 1 + i, X) * (Y * CORES)
-        for d in reach:
+    x, y, cores = parts
+    columns = [lax.rem(x + i, X) * (Y * CORES) for i in (2, 1, 3, 0)]
+
+    def row(i, carry):
+        half, odd = lax.div(i + 1, 2), lax.rem(i, 2)
+        near = lax.rem(y + Y // 2 + half * (1 - 2 * odd), Y) * CORES
+        for column in columns:
             for c in range(CORES):
-                act(base + along[d] + cores[c])
+                act(column + near + cores[c])
         return carry
 
-    lax.fori_loop(0, X - 1, column, 0)
-    for d in reach:
+    lax.fori_loop(0, Y - 1, row, 0)
+    for column in columns[:-1]:
         for c in range(CORES):
-            if d or c:
-                act(x * (Y * CORES) + along[d] + cores[c])
+            act(column + y * CORES + cores[c])
+    act(columns[-1] + y * CORES + cores[1])
 
 
 def rows_of(device):
@@ -216,11 +215,6 @@
     ]
     for load in loads:
         load.start()
-    loads[1].wait()
-    loads[2].wait()
-    gate_key[...] = gate_key[...] * gate_value[...]
-    loads[0].wait()
-
     @pl.when(me == 0)
     def _():
         pl.semaphore_wait(barrier, GROUPS - 1)
@@ -230,6 +224,11 @@
                 here_sem, inc=1, device_id={"seq": peer}, device_id_type=MESH
             ),
         )
+
+    loads[1].wait()
+    loads[2].wait()
+    gate_key[...] = gate_key[...] * gate_value[...]
+    loads[0].wait()
 
     @pl.when(me > 0)
     def _():

time: 51.3 us -> 50.2 us (0.979)
  Pallas kernels: 49.1 us -> 48 us
    pallas_call x1, Pallas kernels: 49.1 us -> 48 us  [body(): pl.pallas_call(kernel, out_shape=(pltpu.VMEM(hyena_query.shape, jnp.float...]
where the time goes in v5:
time: 50.2 us; the launch traced here: 50 us
  Pallas kernels  48 us (96%)
  local copies, waits for them, and re-layouts  1.41 us (3%)
  between operations  0.64 us (1%)
    pallas_call x1, Pallas kernels, body(): pl.pallas_call(kernel, out_shape=(pltpu.VMEM(hyena_query.shape, jnp.float...  48 us
    unnamed x2, local copies, waits for them, and re-layouts  1.41 us

profile of v5, /device:TPU:1, one launch (start us, length us, event | category | flops | bytes accessed | tf_op | source)
XLA Modules:
  0.0 50.0 jit_solution(5302995213027967886)
XLA Ops:
  0.6 48.0 %shard_map.131 = (f32[512,128]{1,0:T(8,128)S(1)}, f32[128,512]{1,0:T(8,128)S(1)}) custom-call(f32[512,128]{1,0:T(8,128)} %query_hbm.1, f32[512,128]{1,0:T(8,128)} %key_hbm.1, f32[512,128]{1,0:T(8,128)} %value_hbm.1, f32[512,128]{1,0:T(8,128)} %filter_hbm.1, f32[128,512]{1,0:T(8,128)} %queries_hbm.1, f32[128,512]{1,0:T(8,128)} %keys_hbm.1, ...), custom_call_target="tpu_custom_call" | custom-call | tf_op jit(solution)/shard_map/pallas_call | solution.py:345
  48.6 0.7 %copy.16 = f32[512,128]{1,0:T(8,128)} copy(f32[512,128]{1,0:T(8,128)S(1)} %get-tuple-element.2) | data formatting | bytes 524288
  49.3 0.7 %copy.17 = f32[128,512]{1,0:T(8,128)} copy(f32[128,512]{1,0:T(8,128)S(1)} %get-tuple-element.3) | data formatting | bytes 524288

commit v6 on v5

--- a/solution.py
+++ b/solution.py
@@ -146,11 +146,33 @@
     act(columns[-1] + y * CORES + cores[1])
 
 
+COLUMNS = (1, 2, 3, 0)
+
+
+def by_column(parts, act):
+    x, y, cores = parts
+
+    def rows(column, least):
+        for far in range(Y // 2, 0, -1):
+            for d in dict.fromkeys((far, Y - far)):
+                for c in range(CORES):
+                    act(column + lax.rem(y + d, Y) * CORES + cores[c])
+        for c in range(least, CORES):
+            act(column + y * CORES + cores[c])
+
+    def other(i, carry):
+        rows(lax.rem(x + 1 + i, X) * (Y * CORES), 0)
+        return carry
+
+    lax.fori_loop(0, X - 1, other, 0)
+    rows(x * (Y * CORES), 1)
+
+
 def rows_of(device):
     return pl.ds(pl.multiple_of(device * CHANNELS, CHANNELS), CHANNELS)
 
 
-def to_all(source, target, me, parts, send_sem, recv_sem, least=0):
+def to_all(source, target, me, parts, send_sem, recv_sem, least=0, others=for_others):
     mine = rows_of(me)
 
     def send(peer):
@@ -158,7 +180,7 @@
         def _():
             start_to(source.at[rows_of(peer), :], target.at[mine, :], peer, send_sem, recv_sem)
 
-    for_others(parts, send)
+    others(parts, send)
     pltpu.make_async_copy(source.at[mine, :], target.at[mine, :], recv_sem).start()
 
 
@@ -279,17 +301,21 @@
 
     signal = to_spectrum(block(got_gate), ahead, twist, forward, high, low)
     multiply_back(signal, spectrum[...], back, twist, inverse, high, low, store)
-    to_all(convolved, got_back, me, parts, all_send.at[2], back_sem.at[parts[0]])
+    to_all(convolved, got_back, me, parts, all_send.at[2], back_sem.at[parts[0]], 0, by_column)
     relay(key_slots, key_sends, key_recvs)
 
+    def in_turn(device):
+        x = lax.div(device, Y * CORES)
+        return [lax.rem(x + X - turn, X) for turn in COLUMNS]
+
     def part(head):
-        rows = pl.ds(head * HEAD_DIM, HEAD_DIM)
+        rows = pl.ds(pl.multiple_of(head * HEAD_DIM, HEAD_DIM), HEAD_DIM)
         slots = [hyena.at[rows, :]] + [values.at[o, rows, :] for o in range(1, span)]
         sends = [value_send.at[o, head] for o in range(span)]
         recvs = [value_recv.at[o, head] for o in range(span)]
         return rows, slots, sends, recvs
 
-    for head in range(heads):
+    for head in in_turn(me):
         rows, slots, sends, recvs = part(head)
         done(got_back.at[rows, :], back_sem.at[head])
         hyena[rows, :] = gate[rows, :] * got_back[rows, :]
@@ -298,25 +324,24 @@
     allowed = [allowed_keys(key_blocks[...], me - o, o, length) for o in range(span)]
     done(key_slots[1], key_recvs[1])
     done(key_slots[3], key_recvs[3])
-    for head in range(heads):
-        cols = slice(head * HEAD_DIM, (head + 1) * HEAD_DIM)
-        query = queries[:, cols] * HEAD_DIM ** (-0.5)
+    for head in in_turn(lax.rem(me + GROUPS - 2, GROUPS)):
+        rows, slots, sends, recvs = part(head)
+        query = queries[:, rows] * HEAD_DIM ** (-0.5)
         scores = [
-            jnp.where(allowed[o], dot_nt(query, keys[o, :, cols], EXACT), -1e30) for o in range(span)
+            jnp.where(allowed[o], dot_nt(query, keys[o, :, rows], EXACT), -1e30) for o in range(span)
         ]
         top = jnp.max(functools.reduce(jnp.maximum, scores), axis=1, keepdims=True)
         expo = [jnp.exp(s - top) for s in scores]
         total = jnp.sum(functools.reduce(jnp.add, expo), axis=1, keepdims=True)
         weight_high[head], weight_low[head] = split(jnp.concatenate(expo, axis=1) / total)
-        rows, slots, sends, recvs = part(head)
         relay(slots, sends, recvs)
 
-    for head in range(heads):
+    for head in in_turn(lax.rem(me + GROUPS - 3, GROUPS)):
         rows, slots, sends, recvs = part(head)
         done(slots[1], recvs[1])
         done(slots[3], recvs[3])
         value_high, value_low = split(jnp.concatenate([slot[...] for slot in slots], axis=1))
-        attended[:, head * HEAD_DIM : (head + 1) * HEAD_DIM] = (
+        attended[:, rows] = (
             dot_nt(weight_high[head], value_high)
             + dot_nt(weight_low[head], value_high)
             + dot_nt(weight_high[head], value_low)
@@ -330,6 +355,17 @@
         for head in range(heads):
             rows, slots, sends, recvs = part(head)
             done(slots[o], sends[o])
+
+
+def write_kernel(hyena, attended, hyena_hbm, attended_hbm, sem):
+    copies = [
+        pltpu.make_async_copy(hyena, hyena_hbm, sem.at[0]),
+        pltpu.make_async_copy(attended, attended_hbm, sem.at[1]),
+    ]
+    for copy in copies:
+        copy.start()
+    for copy in copies:
+        copy.wait()
 
 
 def body(hyena_query, hyena_key, hyena_value, long_filter, queries, keys, key_blocks):
@@ -342,7 +378,7 @@
     dma = pltpu.SemaphoreType.DMA
     rows = CHANNELS * groups
     operands = (hyena_query, hyena_key, hyena_value, long_filter, queries, keys, key_blocks, *tables)
-    return pl.pallas_call(
+    results = pl.pallas_call(
         kernel,
         out_shape=(
             pltpu.VMEM(hyena_query.shape, jnp.float32),
@@ -382,6 +418,14 @@
         ],
         compiler_params=pltpu.CompilerParams(collective_id=0, has_side_effects=True),
     )(*operands)
+    return pl.pallas_call(
+        write_kernel,
+        out_shape=tuple(jax.ShapeDtypeStruct(r.shape, r.dtype) for r in results),
+        in_specs=[pl.BlockSpec(memory_space=pl.ANY)] * 2,
+        out_specs=[pl.BlockSpec(memory_space=pltpu.HBM)] * 2,
+        scratch_shapes=[dma((2,))],
+        compiler_params=pltpu.CompilerParams(vmem_limit_bytes=1 << 20),
+    )(*results)
 
 
 def solution(mesh):

time: 50.2 us -> 49.1 us (0.978)
  local copies, waits for them, and re-layouts: 1.41 us -> 0 us
    unnamed x2 -> x0, local copies, waits for them, and re-layouts: 1.41 us -> none
    pallas_call x1, Pallas kernels: 48 us -> 47.1 us  [body(): pl.pallas_call(kernel, out_shape=(pltpu.VMEM(hyena_query.shape, jnp.float...]
    pallas_call x0 -> x1, Pallas kernels: none -> 0.81 us  [body(): pl.pallas_call(write_kernel, out_shape=tuple((jax.ShapeDtypeStruct(r.shap...]
where the time goes in v6:
time: 49.1 us; the launch traced here: 48.5 us
  Pallas kernels  47.9 us (98%)
  between operations  0.64 us (1%)
    pallas_call x1, Pallas kernels, body(): pl.pallas_call(kernel, out_shape=(pltpu.VMEM(hyena_query.shape, jnp.float...  47.1 us

profile of v6, /device:TPU:1, one launch (start us, length us, event | category | flops | bytes accessed | tf_op | source)
XLA Modules:
  0.0 48.5 jit_solution(6768374874293007949)
XLA Ops:
  0.6 47.1 %shard_map.131 = (f32[512,128]{1,0:T(8,128)S(1)}, f32[128,512]{1,0:T(8,128)S(1)}) custom-call(f32[512,128]{1,0:T(8,128)} %query_hbm.1, f32[512,128]{1,0:T(8,128)} %key_hbm.1, f32[512,128]{1,0:T(8,128)} %value_hbm.1, f32[512,128]{1,0:T(8,128)} %filter_hbm.1, f32[128,512]{1,0:T(8,128)} %queries_hbm.1, f32[128,512]{1,0:T(8,128)} %keys_hbm.1, ...), custom_call_target="tpu_custom_call" | custom-call | tf_op jit(solution)/shard_map/pallas_call | solution.py:381
  47.7 0.8 %shard_map.132 = (f32[512,128]{1,0:T(8,128)}, f32[128,512]{1,0:T(8,128)}) custom-call(f32[512,128]{1,0:T(8,128)S(1)} %get-tuple-element.4.hyena, f32[128,512]{1,0:T(8,128)S(1)} %get-tuple-element.5.attended), custom_call_target="tpu_custom_call" | custom-call | tf_op jit(solution)/shard_map/pallas_call | solution.py:421

commit v7 on v6

--- a/solution.py
+++ b/solution.py
@@ -213,7 +213,6 @@
     me = lax.axis_index("seq")
     parts = terms(me)
     core = parts[2][0]
-    after, later = lax.rem(me + 1, GROUPS), lax.rem(me + 2, GROUPS)
     barrier = pltpu.get_barrier_semaphore()
 
     def greet(peer):
@@ -269,6 +268,13 @@
     for load in loads[3:]:
         load.wait()
 
+    for o in range(1, span):
+
+        @pl.when(me < o)
+        def _():
+            keys[o] = jnp.zeros(keys.shape[1:], jnp.float32)
+            values[o] = jnp.zeros(values.shape[1:], jnp.float32)
+
     def block(ref):
         return lambda k: ref[pl.ds(k, groups, stride=CHANNELS), :]
 
@@ -276,20 +282,48 @@
         convolved[pl.ds(k, groups, stride=CHANNELS), :] = value
 
     def pass_on(own, slots, send_sems, recv_sems):
-        start_to(own, slots[2], later, send_sems[2], recv_sems[2])
+        @pl.when(me < GROUPS - 2)
+        def _():
+            start_to(own, slots[2], me + 2, send_sems[2], recv_sems[2])
 
         @pl.when(core == 0)
         def _():
-            start_to(own, slots[1], after, send_sems[1], recv_sems[1])
+            start_to(own, slots[1], me + 1, send_sems[1], recv_sems[1])
 
     def relay(slots, send_sems, recv_sems):
-        done(slots[2], recv_sems[2])
-
-        @pl.when(core == 1)
-        def _():
-            start_to(slots[2], slots[1], me - 1, send_sems[1], recv_sems[1])
-
-        start_to(slots[2], slots[3], after, send_sems[3], recv_sems[3])
+        @pl.when(me >= 2)
+        def _():
+            done(slots[2], recv_sems[2])
+
+            @pl.when(core == 1)
+            def _():
+                start_to(slots[2], slots[1], me - 1, send_sems[1], recv_sems[1])
+
+            @pl.when(me < GROUPS - 1)
+            def _():
+                start_to(slots[2], slots[3], me + 1, send_sems[3], recv_sems[3])
+
+    def arrived(slots, recv_sems):
+        @pl.when(me >= 1)
+        def _():
+            done(slots[1], recv_sems[1])
+
+        @pl.when(me >= 3)
+        def _():
+            done(slots[3], recv_sems[3])
+
+    def left(slots, send_sems):
+        @pl.when(me < GROUPS - 2)
+        def _():
+            done(slots[2], send_sems[2])
+
+        @pl.when(me != 1)
+        def _():
+            done(slots[1], send_sems[1])
+
+        @pl.when((me >= 2) & (me < GROUPS - 1))
+        def _():
+            done(slots[3], send_sems[3])
 
     key_slots = [keys.at[o] for o in range(span)]
     key_sends = [key_send.at[o] for o in range(span)]
@@ -322,8 +356,7 @@
         pass_on(slots[0], slots, sends, recvs)
 
     allowed = [allowed_keys(key_blocks[...], me - o, o, length) for o in range(span)]
-    done(key_slots[1], key_recvs[1])
-    done(key_slots[3], key_recvs[3])
+    arrived(key_slots, key_recvs)
     for head in in_turn(lax.rem(me + GROUPS - 2, GROUPS)):
         rows, slots, sends, recvs = part(head)
         query = queries[:, rows] * HEAD_DIM ** (-0.5)
@@ -338,8 +371,7 @@
 
     for head in in_turn(lax.rem(me + GROUPS - 3, GROUPS)):
         rows, slots, sends, recvs = part(head)
-        done(slots[1], recvs[1])
-        done(slots[3], recvs[3])
+        arrived(slots, recvs)
         value_high, value_low = split(jnp.concatenate([slot[...] for slot in slots], axis=1))
         attended[:, rows] = (
             dot_nt(weight_high[head], value_high)
@@ -350,11 +382,10 @@
     others = (GROUPS - 1) * CHANNELS
     for i, source in enumerate((taps, gate_key, convolved)):
         done(source.at[pl.ds(0, others), :], all_send.at[i])
-    for o in range(1, span):
-        done(key_slots[o], key_sends[o])
-        for head in range(heads):
-            rows, slots, sends, recvs = part(head)
-            done(slots[o], sends[o])
+    left(key_slots, key_sends)
+    for head in range(heads):
+        rows, slots, sends, recvs = part(head)
+        left(slots, sends)
 
 
 def write_kernel(hyena, attended, hyena_hbm, attended_hbm, sem):

time: 49.1 us -> 46.9 us (0.955)
  the two profiles are of different devices: /device:TPU:1 before, /device:TPU:962 now
where the time goes in v7:
time: 46.9 us; the launch traced here: 46.8 us
  Pallas kernels  46.1 us (98%)
  between operations  0.64 us (1%)
    pallas_call x1, Pallas kernels, body(): pl.pallas_call(kernel, out_shape=(pltpu.VMEM(hyena_query.shape, jnp.float...  45.3 us

profile of v7, /device:TPU:962, one launch (start us, length us, event | category | flops | bytes accessed | tf_op | source)
XLA Modules:
  0.0 46.8 jit_solution(17494009394010375910)
XLA Ops:
  0.6 45.3 %shard_map.131 = (f32[512,128]{1,0:T(8,128)S(1)}, f32[128,512]{1,0:T(8,128)S(1)}) custom-call(f32[512,128]{1,0:T(8,128)} %query_hbm.1, f32[512,128]{1,0:T(8,128)} %key_hbm.1, f32[512,128]{1,0:T(8,128)} %value_hbm.1, f32[512,128]{1,0:T(8,128)} %filter_hbm.1, f32[128,512]{1,0:T(8,128)} %queries_hbm.1, f32[128,512]{1,0:T(8,128)} %keys_hbm.1, ...), custom_call_target="tpu_custom_call" | custom-call | tf_op jit(solution)/shard_map/pallas_call | solution.py:412
  46.0 0.8 %shard_map.132 = (f32[512,128]{1,0:T(8,128)}, f32[128,512]{1,0:T(8,128)}) custom-call(f32[512,128]{1,0:T(8,128)S(1)} %get-tuple-element.4.hyena, f32[128,512]{1,0:T(8,128)S(1)} %get-tuple-element.5.attended), custom_call_target="tpu_custom_call" | custom-call | tf_op jit(solution)/shard_map/pallas_call | solution.py:452

commit v8 on v7

--- a/solution.py
+++ b/solution.py
@@ -147,6 +147,7 @@
 
 
 COLUMNS = (1, 2, 3, 0)
+WRITES = 4
 
 
 def by_column(parts, act):
@@ -389,10 +390,14 @@
 
 
 def write_kernel(hyena, attended, hyena_hbm, attended_hbm, sem):
-    copies = [
-        pltpu.make_async_copy(hyena, hyena_hbm, sem.at[0]),
-        pltpu.make_async_copy(attended, attended_hbm, sem.at[1]),
-    ]
+    copies = []
+    for source, target in ((attended, attended_hbm), (hyena, hyena_hbm)):
+        size = source.shape[0] // WRITES
+        for i in range(WRITES):
+            rows = pl.ds(i * size, size)
+            copies.append(
+                pltpu.make_async_copy(source.at[rows, :], target.at[rows, :], sem.at[len(copies)])
+            )
     for copy in copies:
         copy.start()
     for copy in copies:
@@ -454,7 +459,7 @@
         out_shape=tuple(jax.ShapeDtypeStruct(r.shape, r.dtype) for r in results),
         in_specs=[pl.BlockSpec(memory_space=pl.ANY)] * 2,
         out_specs=[pl.BlockSpec(memory_space=pltpu.HBM)] * 2,
-        scratch_shapes=[dma((2,))],
+        scratch_shapes=[dma((2 * WRITES,))],
         compiler_params=pltpu.CompilerParams(vmem_limit_bytes=1 << 20),
     )(*results)
 

time: 46.9 us -> 47 us (level)
  the two profiles are of different devices: /device:TPU:962 before, /device:TPU:386 now
where the time goes in v8:
time: 47 us; the launch traced here: 46.8 us
  Pallas kernels  46.2 us (98%)
  between operations  0.64 us (1%)
    pallas_call x1, Pallas kernels, body(): pl.pallas_call(kernel, out_shape=(pltpu.VMEM(hyena_query.shape, jnp.float...  45.3 us

profile of v8, /device:TPU:386, one launch (start us, length us, event | category | flops | bytes accessed | tf_op | source)
XLA Modules:
  0.0 46.8 jit_solution(2947116647977405751)
XLA Ops:
  0.6 45.3 %shard_map.131 = (f32[512,128]{1,0:T(8,128)S(1)}, f32[128,512]{1,0:T(8,128)S(1)}) custom-call(f32[512,128]{1,0:T(8,128)} %query_hbm.1, f32[512,128]{1,0:T(8,128)} %key_hbm.1, f32[512,128]{1,0:T(8,128)} %value_hbm.1, f32[512,128]{1,0:T(8,128)} %filter_hbm.1, f32[128,512]{1,0:T(8,128)} %queries_hbm.1, f32[128,512]{1,0:T(8,128)} %keys_hbm.1, ...), custom_call_target="tpu_custom_call" | custom-call | tf_op jit(solution)/shard_map/pallas_call | solution.py:417
  46.0 0.9 %shard_map.132 = (f32[512,128]{1,0:T(8,128)}, f32[128,512]{1,0:T(8,128)}) custom-call(f32[512,128]{1,0:T(8,128)S(1)} %get-tuple-element.4.hyena, f32[128,512]{1,0:T(8,128)S(1)} %get-tuple-element.5.attended), custom_call_target="tpu_custom_call" | custom-call | tf_op jit(solution)/shard_map/pallas_call | solution.py:457
